TPU v7x, 256 devices: a whole 4x4x8 slice. The times are simulated.
256 devices in a mesh: dp: 4 (over y), expert: 64 (over x, z, core).
Axes of the slice: x: 4, y: 4, z: 8, core: 2. Of those that a mesh axis runs over, the one named last changes fastest.
Arguments:
- tokens: bfloat16 [8192, 7168], P('expert', 'dp'), may hold values from -6 to 6
- route_ids: int32 [8192, 8], P('expert'), may hold values from 0 to 63, all different within a row; in each aligned block of 128 rows (0 to 127, 128 to 255, ...) at most 20 rows name the same one
- route_weights: float32 [8192, 8], P('expert'), may hold values from 0.1 to 0.6
- swap_flags: int32 [64], replicated, may hold values from 0 to 1, as said below
- gate_weight: bfloat16 [64, 7168, 1024], P('expert', 'dp'), may hold values from -0.0625 to 0.0625
- up_weight: bfloat16 [64, 7168, 1024], P('expert', 'dp'), may hold values from -0.0625 to 0.0625
- down_weight: bfloat16 [64, 1024, 7168], P('expert', None, 'dp'), may hold values from -0.1875 to 0.1875
Outputs:
- mixed: bfloat16 [8192, 7168], P('expert', 'dp')
Inputs may be any that keep to these rules, and one draw needn't show every extreme that they name: `route_ids`: each row names 8 different slots. In each aligned block of 128 rows (the rows of one device along `expert`) no slot is named by more than 20 rows, a bound that some block reaches. swap_flags[s] equals swap_flags[(s + 32) mod 64] for every slot s; swap_flags[0] and swap_flags[31] are 1 and swap_flags[1] is 0.
All inputs are finite; a program needn't handle non-finite values.
Results may differ from a plain program's by a relative error of at most 0.019.
Values may be sent and summed in bfloat16 or wider, within the bound.
No kernel may reach another device: no remote copies, remote signals or barrier semaphores. Data moves between devices by JAX's collectives and lax.ppermute only.
A program may use at most 128 MiB of HBM per device.

v0:
```python
import jax
import jax.numpy as jnp
from jax import lax
from jax.sharding import PartitionSpec as P


def shifted(x, axis, by):
    devices = lax.axis_size(axis)
    return lax.ppermute(x, axis, [(i, (i + by) % devices) for i in range(devices)])


def per_device(tokens, route_ids, route_weights, swap_flags, gate_weight, up_weight, down_weight):
    experts = lax.axis_size("expert")
    tok_rows, quarter = tokens.shape
    choices_per = route_ids.shape[1]
    hidden = gate_weight.shape[2]
    capacity = max(2, min(tok_rows, 5 * tok_rows * choices_per // (4 * experts)))
    w_gate = gate_weight[0]
    w_up = up_weight[0]
    w_down = down_weight[0]
    theirs = shifted((w_gate, w_up, w_down), "expert", experts // 2)
    swapped_here = swap_flags[lax.axis_index("expert")] == 1
    w_gate = jnp.where(swapped_here, theirs[0], w_gate)
    w_up = jnp.where(swapped_here, theirs[1], w_up)
    w_down = jnp.where(swapped_here, theirs[2], w_down)
    flat_ids = route_ids.reshape(-1)
    onehot = (flat_ids[:, None] == jnp.arange(experts, dtype=jnp.int32)[None, :]).astype(jnp.int32)
    running = jnp.cumsum(onehot, axis=0) - onehot
    rank_in = jnp.sum(running * onehot, axis=1)
    slot_of = flat_ids * capacity + rank_in
    entry_count = flat_ids.shape[0]
    slot_table = (
        jnp.zeros((experts * capacity,), jnp.int32)
        .at[slot_of]
        .set(jnp.arange(entry_count, dtype=jnp.int32) + 1)
    )
    filled = slot_table > 0
    source_tok = jnp.maximum(slot_table - 1, 0) // choices_per
    gathered = tokens[source_tok]
    outgoing = jnp.where(filled[:, None], gathered, jnp.zeros_like(gathered)).reshape(
        experts, capacity, quarter
    )
    arrived = lax.all_to_all(outgoing, "expert", split_axis=0, concat_axis=0, tiled=True)
    all_rows = arrived.reshape(experts * capacity, quarter)
    gate_term = jnp.dot(all_rows, w_gate, preferred_element_type=jnp.float32)
    up_term = jnp.dot(all_rows, w_up, preferred_element_type=jnp.float32)
    summed = lax.psum_scatter(
        jnp.concatenate([gate_term, up_term], axis=1).astype(jnp.bfloat16),
        "dp",
        scatter_dimension=0,
        tiled=True,
    ).astype(jnp.float32)
    activated = (jax.nn.silu(summed[:, :hidden]) * summed[:, hidden:]).astype(jnp.bfloat16)
    results = jnp.dot(
        lax.all_gather(activated, "dp", axis=0, tiled=True),
        w_down,
        preferred_element_type=jnp.float32,
    )
    leaving = results.astype(jnp.bfloat16).reshape(experts, capacity, quarter)
    returned = lax.all_to_all(leaving, "expert", split_axis=0, concat_axis=0, tiled=True)
    returned_flat = returned.reshape(experts * capacity, quarter)
    picked = returned_flat[slot_of].reshape(tok_rows, choices_per, quarter)
    mixed = jnp.sum(route_weights[:, :, None] * picked.astype(jnp.float32), axis=1)
    return mixed.astype(jnp.bfloat16)


def solution(mesh):
    in_specs = (
        P("expert", "dp"),
        P("expert", None),
        P("expert", None),
        P(),
        P("expert", "dp", None),
        P("expert", "dp", None),
        P("expert", None, "dp"),
    )
    out_specs = P("expert", "dp")
    return jax.shard_map(
        per_device, mesh=mesh, in_specs=in_specs, out_specs=out_specs, check_vma=False
    )
```

profile of v0, /device:TPU:1, one launch (start us, length us, event | category | flops | bytes accessed | tf_op | source)
XLA Modules:
  0.0 629.1 jit_solution(14425553313564526043)
XLA Ops:
  6.5 0.0 copy-start
  6.5 0.8 copy.17
  7.4 0.1 eq.35
  7.5 0.1 eq.31
  7.6 0.7 broadcast_multiply_fusion
  8.3 18.0 %reduce-window.6 = s32[64,8,128]{2,1,0:T(8,128)S(1)} reduce-window(s32[64,8,128]{2,1,0:T(8,128)S(1)} %fusion.11, s32[]{:T(128)} %constant.18.clone.1), window={size=1x1x128 pad=0_0x0_0x127_0}, to_apply=%region_0.1 | reduce-window | flops 8323072 | bytes 524292 | tf_op jit(solution)/shard_map/reduce-window
  26.3 0.1 slice.20
  26.4 0.1 copy.19
  26.6 0.1 copy.20
  26.7 0.1 broadcast_add_fusion
  26.8 0.1 copy.16
  26.9 0.1 mul.37
  27.0 0.1 fusion.10
  27.1 4.3 scatter_custom_fusion
  31.5 0.0 copy-done
  31.5 5.8 gather_fusion
  37.3 7.3 %gather.9 = bf16[64,20,1792]{2,1,0:T(8,128)(2,1)} reshape(bf16[1280,1792]{1,0:T(8,128)(2,1)} %gather_fusion) | data formatting | bytes 9175040 | tf_op jit(solution)/shard_map/gather | solution.py:39
  44.5 0.1 broadcast_in_dim.21
  44.7 5.5 broadcast_select_fusion
  50.1 0.0 copy-start.5
  50.1 13.3 %all-to-all-start = ((bf16[64,20,1792]{2,1,0:T(8,128)(2,1)}), bf16[64,20,1792]{2,1,0:T(8,128)(2,1)}, u32[]{:S(2)}, u32[]{:S(2)}) async-start(bf16[64,20,1792]{2,1,0:T(8,128)(2,1)} %broadcast_select_fusion), calls=%async_computation | async-start | bytes 11010048 | tf_op jit(solution)/shard_map/all_to_all | solution.py:43
  63.4 0.0 reduce-scatter.4.cloned.1.call-start
  63.5 3.0 collective-permute-start
  66.5 0.3 collective-permute-start.1
  66.8 0.0 copy-done.5
  66.8 0.6 dynamic_slice.3
  68.0 119.3 %all-to-all-done = bf16[64,20,1792]{2,1,0:T(8,128)(2,1)} async-done(((bf16[64,20,1792]{2,1,0:T(8,128)(2,1)}), bf16[64,20,1792]{2,1,0:T(8,128)(2,1)}, u32[]{:S(2)}, u32[]{:S(2)}) %all-to-all-start) | async-done | bytes 4587552 | tf_op jit(solution)/shard_map/all_to_all | solution.py:43
  187.4 7.3 %reshape.70 = bf16[1280,1792]{1,0:T(8,128)(2,1)} reshape(bf16[64,20,1792]{2,1,0:T(8,128)(2,1)} %all-to-all-done) | data formatting | bytes 9175040 | tf_op jit(solution)/shard_map/reshape | solution.py:44
  194.6 10.7 %collective-permute-done = bf16[1792,1024]{1,0:T(8,128)(2,1)} collective-permute-done((bf16[1792,1024]{1,0:T(8,128)(2,1)}, bf16[1792,1024]{1,0:T(8,128)(2,1)}, u32[]{:S(2)}, u32[]{:S(2)}) %collective-permute-start) | collective-permute-done | bytes 3670048 | tf_op jit(solution)/shard_map/ppermute | solution.py:9
  205.3 0.0 copy-start.2
  205.3 0.0 copy-start.4
  205.3 8.8 %convolution_convert_fusion.2 = bf16[1280,1024]{0,1:T(8,128)(2,1)S(1)} fusion(bf16[1280,1792]{1,0:T(8,128)(2,1)} %reshape.70, bf16[1792,1024]{1,0:T(8,128)(2,1)} %collective-permute-done, pred[]{:T(512)} %bitcast.4, bf16[1,1792,1024]{2,1,0:T(8,128)(2,1)} %param.11), kind=kOutput, calls=%fused_computation.9 | convolution fusion | flops 4700766208 | bytes 14548993 | tf_op jit(solution)/shard_map/dot_general | solution.py:45
  214.1 69.9 %collective-permute-done.1 = bf16[1792,1024]{1,0:T(8,128)(2,1)} collective-permute-done((bf16[1792,1024]{1,0:T(8,128)(2,1)}, bf16[1792,1024]{1,0:T(8,128)(2,1)}, u32[]{:S(2)}, u32[]{:S(2)}) %collective-permute-start.1) | collective-permute-done | bytes 3670048 | tf_op jit(solution)/shard_map/ppermute | solution.py:9
  284.0 0.0 copy-done.2
  284.0 0.0 copy-done.4
  284.0 5.6 convolution_convert_fusion.1
  289.6 2.7 pad_maximum_fusion
  292.3 8.0 %copy.22 = bf16[1280,2048]{1,0:T(8,128)(2,1)} copy(bf16[1280,2048]{0,1:T(8,128)(2,1)} %pad_maximum_fusion) | data formatting | bytes 10485760
  300.2 0.0 reduce-scatter.4.cloned.1.call-update
  300.3 0.3 all-gather.2.cloned.1.call-start
  300.5 58.8 %reduce-scatter.4.cloned.1.call-done = bf16[320,2048]{1,0:T(8,128)(2,1)} async-done(((bf16[1280,2048]{1,0:T(8,128)(2,1)}), bf16[320,2048]{1,0:T(8,128)(2,1)}) %reduce-scatter.4.cloned.1.call-update) | async-done | bytes 1310736
  359.3 1.8 copy.23
  361.2 0.2 convert_element_type.28
  361.4 0.5 fusion.7
  361.8 1.1 copy.21
  363.0 0.0 all-gather.2.cloned.1.call-update
  363.0 2.8 collective-permute-start.2
  365.8 79.3 %collective-permute-done.2 = bf16[1024,1792]{1,0:T(8,128)(2,1)} collective-permute-done((bf16[1024,1792]{1,0:T(8,128)(2,1)}, bf16[1024,1792]{1,0:T(8,128)(2,1)}, u32[]{:S(2)}, u32[]{:S(2)}) %collective-permute-start.2) | collective-permute-done | bytes 3670048 | tf_op jit(solution)/shard_map/ppermute | solution.py:9
  445.0 0.0 all-gather.2.cloned.1.call-done
  445.0 9.8 %convolution_convert_fusion = bf16[1280,1792]{1,0:T(8,128)(2,1)} fusion(bf16[1280,1024]{1,0:T(8,128)(2,1)} %all-gather.2.cloned.1.call-done, bf16[1024,1792]{1,0:T(8,128)(2,1)} %collective-permute-done.2, pred[]{:T(512)} %bitcast.4, bf16[1,1024,1792]{2,1,0:T(8,128)(2,1)} %param.13), kind=kOutput, calls=%fused_computation.3 | convolution fusion | flops 4701749248 | bytes 14548993 | tf_op jit(solution)/shard_map/dot_general | solution.py:54
  454.9 7.3 %reshape.71 = bf16[64,20,1792]{2,1,0:T(8,128)(2,1)} reshape(bf16[1280,1792]{1,0:T(8,128)(2,1)} %convolution_convert_fusion) | data formatting | bytes 9175040 | tf_op jit(solution)/shard_map/reshape | solution.py:59
  462.1 0.0 copy-start.3
  462.1 11.9 %all-to-all-start.1 = ((bf16[64,20,1792]{2,1,0:T(8,128)(2,1)}), bf16[64,20,1792]{2,1,0:T(8,128)(2,1)}, u32[]{:S(2)}, u32[]{:S(2)}) async-start(bf16[64,20,1792]{2,1,0:T(8,128)(2,1)} %reshape.71), calls=%async_computation.1 | async-start | bytes 11010048 | tf_op jit(solution)/shard_map/all_to_all | solution.py:60
  474.0 0.0 copy-done.3
  474.0 0.1 copy.15
  474.1 123.8 %all-to-all-done.1 = bf16[64,20,1792]{2,1,0:T(8,128)(2,1)} async-done(((bf16[64,20,1792]{2,1,0:T(8,128)(2,1)}), bf16[64,20,1792]{2,1,0:T(8,128)(2,1)}, u32[]{:S(2)}, u32[]{:S(2)}) %all-to-all-start.1) | async-done | bytes 4587552 | tf_op jit(solution)/shard_map/all_to_all | solution.py:60
  598.0 7.3 %reshape.72 = bf16[1280,1792]{1,0:T(8,128)(2,1)} reshape(bf16[64,20,1792]{2,1,0:T(8,128)(2,1)} %all-to-all-done.1) | data formatting | bytes 9175040 | tf_op jit(solution)/shard_map/reshape | solution.py:61
  605.2 0.0 copy-start.1
  605.2 10.9 %gather_fusion.1 = bf16[1024,1792]{1,0:T(8,128)(2,1)} fusion(bf16[1280,1792]{1,0:T(8,128)(2,1)} %reshape.72, s32[1024]{0:T(1024)S(1)} %broadcast_clamp_fusion), kind=kCustom, calls=%fused_computation.1 | custom fusion | bytes 7344128 | tf_op jit(solution)/shard_map/gather | solution.py:62
  616.1 6.1 fusion
  622.2 0.0 copy-done.1
  (9 shorter events, 0.1 us)
Async XLA Ops:
  6.5 25.0 %copy-start = (bf16[128,1792]{1,0:T(8,128)(2,1)S(1)}, bf16[128,1792]{1,0:T(8,128)(2,1)}, u32[]{:S(2)}) copy-start(bf16[128,1792]{1,0:T(8,128)(2,1)} %param.7) | copy-start | bytes 1376260
  50.1 16.7 %copy-start.5 = (s32[64]{0:T(128)S(1)}, s32[64]{0:T(128)}, u32[]{:S(2)}) copy-start(s32[64]{0:T(128)} %param.10) | copy-start | bytes 772
  50.1 137.2 %all-to-all-start = ((bf16[64,20,1792]{2,1,0:T(8,128)(2,1)}), bf16[64,20,1792]{2,1,0:T(8,128)(2,1)}, u32[]{:S(2)}, u32[]{:S(2)}) async-start(bf16[64,20,1792]{2,1,0:T(8,128)(2,1)} %broadcast_select_fusion), calls=%async_computation | async-start | bytes 11010048 | tf_op jit(solution)/shard_map/all_to_all | solution.py:43
  63.4 295.9 %reduce-scatter.4.cloned.1.call-start = ((), (), s32[]{:S(2)}) async-start(), calls=%async_computation.4 | async-start | bytes 6553600
  63.5 141.9 %collective-permute-start = (bf16[1792,1024]{1,0:T(8,128)(2,1)}, bf16[1792,1024]{1,0:T(8,128)(2,1)}, u32[]{:S(2)}, u32[]{:S(2)}) collective-permute-start(bf16[1792,1024]{1,0:T(8,128)(2,1)} %bitcast.48), channel_id=1, source_target_pairs={{0,32},{1,33},{2,34},{3,35},{4,36},{5,37},{6,38},{7,39},{8,40},{9,... | collective-permute-start | bytes 11010056 | tf_op jit(solution)/shard_map/ppermute | solution.py:9
  66.5 217.5 %collective-permute-start.1 = (bf16[1792,1024]{1,0:T(8,128)(2,1)}, bf16[1792,1024]{1,0:T(8,128)(2,1)}, u32[]{:S(2)}, u32[]{:S(2)}) collective-permute-start(bf16[1792,1024]{1,0:T(8,128)(2,1)} %bitcast.49), channel_id=1, source_target_pairs={{0,32},{1,33},{2,34},{3,35},{4,36},{5,37},{6,38},{7,39},{8,40},{9,... | collective-permute-start | bytes 11010056 | tf_op jit(solution)/shard_map/ppermute | solution.py:9
  205.3 78.7 %copy-start.2 = (bf16[1280,1792]{1,0:T(8,128)(2,1)S(1)}, bf16[1280,1792]{1,0:T(8,128)(2,1)}, u32[]{:S(2)}) copy-start(bf16[1280,1792]{1,0:T(8,128)(2,1)} %reshape.70) | copy-start | bytes 13762564
  205.3 78.7 %copy-start.4 = (bf16[1,1792,1024]{2,1,0:T(8,128)(2,1)S(1)}, bf16[1,1792,1024]{2,1,0:T(8,128)(2,1)}, u32[]{:S(2)}) copy-start(bf16[1,1792,1024]{2,1,0:T(8,128)(2,1)} %param.12) | copy-start | bytes 11010052
  300.3 144.8 %all-gather.2.cloned.1.call-start = ((), (), s32[]{:S(2)}) async-start(), calls=%async_computation.3 | async-start | bytes 3276800 | tf_op jit(solution)/shard_map/all_gather | solution.py:55
  363.0 82.1 %collective-permute-start.2 = (bf16[1024,1792]{1,0:T(8,128)(2,1)}, bf16[1024,1792]{1,0:T(8,128)(2,1)}, u32[]{:S(2)}, u32[]{:S(2)}) collective-permute-start(bf16[1024,1792]{1,0:T(8,128)(2,1)} %bitcast.50), channel_id=1, source_target_pairs={{0,32},{1,33},{2,34},{3,35},{4,36},{5,37},{6,38},{7,39},{8,40},{9,... | collective-permute-start | bytes 11010056 | tf_op jit(solution)/shard_map/ppermute | solution.py:9
  462.1 11.9 %copy-start.3 = (f32[128,8]{0,1:T(8,128)S(1)}, f32[128,8]{0,1:T(8,128)}, u32[]{:S(2)}) copy-start(f32[128,8]{0,1:T(8,128)} %param.9) | copy-start | bytes 12292
  462.1 135.8 %all-to-all-start.1 = ((bf16[64,20,1792]{2,1,0:T(8,128)(2,1)}), bf16[64,20,1792]{2,1,0:T(8,128)(2,1)}, u32[]{:S(2)}, u32[]{:S(2)}) async-start(bf16[64,20,1792]{2,1,0:T(8,128)(2,1)} %reshape.71), calls=%async_computation.1 | async-start | bytes 11010048 | tf_op jit(solution)/shard_map/all_to_all | solution.py:60
  605.2 17.0 %copy-start.1 = (bf16[128,1792]{1,0:T(8,128)(2,1)S(1)}, bf16[128,1792]{1,0:T(8,128)(2,1)}, u32[]{:S(2)}) copy-start(bf16[128,1792]{1,0:T(8,128)(2,1)} %param.7) | copy-start | bytes 1376260
Sparse Core Ops, SparseCore 0:
  300.4 58.9 reduce-scatter.3
  363.1 37.3 all-gather.1
where the time goes:
time: 630 us; the launch traced here: 629 us
  waiting for transfers between devices  462 us (73%)
  local copies, waits for them, and re-layouts  63.3 us (10%)
  other arithmetic  33.9 us (5%)
  starting transfers between devices  31.6 us (5%)
  matrix products  24.2 us (4%)
  between operations  14.2 us (2%)
    ppermute x3, waiting for transfers between devices, shifted(): lax.ppermute(x, axis, [(i, (i + by) % devices) for i in range(devices)])  160 us
    all_to_all x1, waiting for transfers between devices, per_device(): lax.all_to_all(leaving, 'expert', split_axis=0, concat_axis=0, tiled=True)  124 us
    all_to_all x1, waiting for transfers between devices, per_device(): lax.all_to_all(outgoing, 'expert', split_axis=0, concat_axis=0, tiled=True)  119 us
    unnamed x3, waiting for transfers between devices  58.8 us
    another operation x3, other arithmetic  18.2 us
    all_to_all x1, starting transfers between devices, per_device(): lax.all_to_all(outgoing, 'expert', split_axis=0, concat_axis=0, tiled=True)  13.3 us
    gather x2, local copies, waits for them, and re-layouts, per_device(): gathered = tokens[source_tok]  13 us
  transfers between devices with their start and end apart: 7, of which 6 were waited for; matrix products, arithmetic and copies ran while one was open for 3% of the time, Pallas kernels for 0%

commit v1 on v0

--- a/solution.py
+++ b/solution.py
@@ -18,12 +18,9 @@
     w_gate = gate_weight[0]
     w_up = up_weight[0]
     w_down = down_weight[0]
-    theirs = shifted((w_gate, w_up, w_down), "expert", experts // 2)
-    swapped_here = swap_flags[lax.axis_index("expert")] == 1
-    w_gate = jnp.where(swapped_here, theirs[0], w_gate)
-    w_up = jnp.where(swapped_here, theirs[1], w_up)
-    w_down = jnp.where(swapped_here, theirs[2], w_down)
-    flat_ids = route_ids.reshape(-1)
+    slots = jnp.arange(experts, dtype=jnp.int32)
+    slot_source = jnp.where(swap_flags == 1, (slots + experts // 2) % experts, slots)
+    flat_ids = slot_source[route_ids.reshape(-1)]
     onehot = (flat_ids[:, None] == jnp.arange(experts, dtype=jnp.int32)[None, :]).astype(jnp.int32)
     running = jnp.cumsum(onehot, axis=0) - onehot
     rank_in = jnp.sum(running * onehot, axis=1)

time: 630 us -> 541 us (0.86)
  waiting for transfers between devices: 462 us -> 216 us
  blocking collectives: 0 us -> 137 us
  other arithmetic: 33.9 us -> 72.1 us
  starting transfers between devices: 31.6 us -> 11.4 us
    ppermute x3 -> x0, waiting for transfers between devices: 160 us -> none  [shifted(): lax.ppermute(x, axis, [(i, (i + by) % devices) for i in range(devices)])]
    all_to_all x0 -> x1, blocking collectives: none -> 137 us  [per_device(): lax.all_to_all(outgoing, 'expert', split_axis=0, concat_axis=0, tiled=True)]
    all_to_all x1 -> x0, waiting for transfers between devices: 119 us -> none  [per_device(): lax.all_to_all(outgoing, 'expert', split_axis=0, concat_axis=0, tiled=True)]
    gather x0 -> x3, other arithmetic: none -> 40.6 us  [per_device(): flat_ids = slot_source[route_ids.reshape(-1)]]
    all_gather x1, waiting for transfers between devices: 0.01 us -> 37.5 us  [per_device(): lax.all_gather(activated, 'dp', axis=0, tiled=True)]
    all_to_all x1 -> x0, starting transfers between devices: 13.3 us -> none  [per_device(): lax.all_to_all(outgoing, 'expert', split_axis=0, concat_axis=0, tiled=True)]
  transfers between devices with their start and end apart: 7 -> 3, of which waited for: 6 -> 3; matrix products, arithmetic and copies ran while one was open for 3% -> 0% of each run, Pallas kernels for 0% -> 0%
where the time goes in v1:
time: 541 us; the launch traced here: 539 us
  waiting for transfers between devices  216 us (40%)
  blocking collectives  137 us (25%)
  other arithmetic  72.1 us (13%)
  local copies, waits for them, and re-layouts  65.2 us (12%)
  matrix products  23.9 us (4%)
  between operations  13.6 us (3%)
  starting transfers between devices  11.4 us (2%)
    all_to_all x1, blocking collectives, per_device(): lax.all_to_all(outgoing, 'expert', split_axis=0, concat_axis=0, tiled=True)  137 us
    all_to_all x1, waiting for transfers between devices, per_device(): lax.all_to_all(leaving, 'expert', split_axis=0, concat_axis=0, tiled=True)  124 us
    unnamed x3, waiting for transfers between devices  54.8 us
    gather x3, other arithmetic, per_device(): flat_ids = slot_source[route_ids.reshape(-1)]  40.6 us
    all_gather x1, waiting for transfers between devices, per_device(): lax.all_gather(activated, 'dp', axis=0, tiled=True)  37.5 us
    another operation x3, other arithmetic  18.2 us
    gather x2, local copies, waits for them, and re-layouts, per_device(): gathered = tokens[source_tok]  13 us
    all_to_all x1, starting transfers between devices, per_device(): lax.all_to_all(leaving, 'expert', split_axis=0, concat_axis=0, tiled=True)  11.1 us
  transfers between devices with their start and end apart: 3, of which 3 were waited for; matrix products, arithmetic and copies ran while one was open for 0% of the time, Pallas kernels for 0%

profile of v1, /device:TPU:1, one launch (start us, length us, event | category | flops | bytes accessed | tf_op | source)
XLA Modules:
  0.0 539.2 jit_solution(5117347892708952578)
XLA Ops:
  6.5 0.0 copy-start
  6.5 0.0 reduce-scatter.4.cloned.1.call-start
  6.5 0.7 compare_select_fusion.11
  7.3 0.7 fusion.15
  8.0 0.7 fusion.16
  8.7 0.7 fusion.13
  9.4 0.7 fusion.14
  10.1 0.8 copy.14
  10.9 0.1 reshape.94
  11.0 4.3 compare_select_fusion.3
  15.3 0.7 compare_reduce_fusion.56
  16.0 35.6 %select_select_fusion = s32[1024]{0:T(1024)S(1)} fusion(pred[1024]{0:T(1024)(128)(4,1)S(1)} %get-tuple-element.61, pred[1024]{0:T(1024)(128)(4,1)S(1)} %get-tuple-element.60, pred[1024]{0:T(1024)(128)(4,1)S(1)} %get-tuple-element.59, pred[1024]{0:T(1024)(128)(4,1)S(1)} %get-tuple-element.58, pred[1024]{0:T(1024)(128)(4,1)S(1)} %get-tuple-element.57, ...), kind=kLoop, calls=%fused_computation.95 | loop fusion | flops 58368 | bytes 66788 | tf_op jit(solution)/shard_map/gather | solution.py:23
  51.7 18.0 %reduce-window.6 = s32[64,8,128]{2,1,0:T(8,128)S(1)} reduce-window(s32[64,8,128]{2,1,0:T(8,128)S(1)} %fusion.8, s32[]{:T(128)} %constant.45.clone.1), window={size=1x1x128 pad=0_0x0_0x127_0}, to_apply=%region_0.1 | reduce-window | flops 8323072 | bytes 524292 | tf_op jit(solution)/shard_map/reduce-window
  69.7 0.1 slice.85
  69.8 0.1 copy.15
  70.0 0.1 copy.16
  70.1 0.1 broadcast_add_fusion
  70.2 0.1 fusion.7
  70.3 4.3 scatter_custom_fusion
  74.7 0.0 copy-done
  74.7 5.8 %gather_fusion = bf16[1280,1792]{1,0:T(8,128)(2,1)} fusion(bf16[128,1792]{1,0:T(8,128)(2,1)S(1)} %copy-done, s32[2048]{0:T(1024)S(1)} %pad_clamp_fusion), kind=kCustom, calls=%fused_computation | custom fusion | bytes 9180160 | tf_op jit(solution)/shard_map/gather | solution.py:36
  80.5 7.2 %gather.13 = bf16[64,20,1792]{2,1,0:T(8,128)(2,1)} reshape(bf16[1280,1792]{1,0:T(8,128)(2,1)} %gather_fusion) | data formatting | bytes 9175040 | tf_op jit(solution)/shard_map/gather | solution.py:36
  87.8 0.1 broadcast_in_dim.14
  87.9 3.0 broadcast_select_fusion
  90.9 136.9 %all_to_all.10 = bf16[64,20,1792]{2,1,0:T(8,128)(2,1)} all-to-all(bf16[64,20,1792]{2,1,0:T(8,128)(2,1)S(1)} %broadcast_select_fusion), channel_id=1, replica_groups=mesh['dp'=4,'expert'=64] {'expert'}, dimensions={0} | all-to-all | bytes 9175040 | tf_op jit(solution)/shard_map/all_to_all | solution.py:40
  227.8 7.2 %reshape.96 = bf16[1280,1792]{1,0:T(8,128)(2,1)} reshape(bf16[64,20,1792]{2,1,0:T(8,128)(2,1)} %all_to_all.10) | data formatting | bytes 9175040 | tf_op jit(solution)/shard_map/reshape | solution.py:41
  235.0 0.0 copy-start.2
  235.0 0.0 copy-start.4
  235.1 8.6 %convolution_convert_fusion.1 = bf16[1280,1024]{0,1:T(8,128)(2,1)S(1)} fusion(bf16[1280,1792]{1,0:T(8,128)(2,1)} %reshape.96, bf16[1,1792,1024]{2,1,0:T(8,128)(2,1)} %param.12), kind=kOutput, calls=%fused_computation.8 | convolution fusion | flops 4698931200 | bytes 10878976 | tf_op jit(solution)/shard_map/dot_general | solution.py:43
  243.6 0.0 copy-done.2
  243.6 0.0 copy-done.4
  243.6 5.5 %convolution_convert_fusion.2 = bf16[1280,1024]{0,1:T(8,128)(2,1)S(1)} fusion(bf16[1280,1792]{1,0:T(8,128)(2,1)S(1)} %copy-done.2, bf16[1,1792,1024]{2,1,0:T(8,128)(2,1)S(1)} %copy-done.4), kind=kOutput, calls=%fused_computation.9 | convolution fusion | flops 4698931200 | bytes 10878976 | tf_op jit(solution)/shard_map/dot_general | solution.py:42
  249.1 2.7 pad_maximum_fusion
  251.8 7.9 %copy.18 = bf16[1280,2048]{1,0:T(8,128)(2,1)} copy(bf16[1280,2048]{0,1:T(8,128)(2,1)} %pad_maximum_fusion) | data formatting | bytes 10485760
  259.7 0.0 reduce-scatter.4.cloned.1.call-update
  259.8 0.3 all-gather.2.cloned.1.call-start
  260.0 54.8 %reduce-scatter.4.cloned.1.call-done = bf16[320,2048]{1,0:T(8,128)(2,1)} async-done(((bf16[1280,2048]{1,0:T(8,128)(2,1)}), bf16[320,2048]{1,0:T(8,128)(2,1)}) %reduce-scatter.4.cloned.1.call-update) | async-done | bytes 1310736
  314.8 1.8 copy.19
  316.7 0.2 convert_element_type.28
  316.9 0.5 fusion.4
  317.3 1.1 copy.17
  318.5 0.0 all-gather.2.cloned.1.call-update
  318.5 37.5 %all-gather.2.cloned.1.call-done = bf16[1280,1024]{1,0:T(8,128)(2,1)} async-done(((bf16[320,1024]{1,0:T(8,128)(2,1)}), bf16[1280,1024]{1,0:T(8,128)(2,1)}) %all-gather.2.cloned.1.call-update) | async-done | bytes 2621456 | tf_op jit(solution)/shard_map/all_gather | solution.py:52
  356.0 9.8 %convolution_convert_fusion = bf16[1280,1792]{1,0:T(8,128)(2,1)} fusion(bf16[1280,1024]{1,0:T(8,128)(2,1)} %all-gather.2.cloned.1.call-done, bf16[1,1024,1792]{2,1,0:T(8,128)(2,1)} %param.13), kind=kOutput, calls=%fused_computation.3 | convolution fusion | flops 4699914240 | bytes 10878976 | tf_op jit(solution)/shard_map/dot_general | solution.py:51
  365.8 7.3 %reshape.97 = bf16[64,20,1792]{2,1,0:T(8,128)(2,1)} reshape(bf16[1280,1792]{1,0:T(8,128)(2,1)} %convolution_convert_fusion) | data formatting | bytes 9175040 | tf_op jit(solution)/shard_map/reshape | solution.py:56
  373.0 0.0 copy-start.3
  373.0 11.1 %all-to-all-start.1 = ((bf16[64,20,1792]{2,1,0:T(8,128)(2,1)}), bf16[64,20,1792]{2,1,0:T(8,128)(2,1)}, u32[]{:S(2)}, u32[]{:S(2)}) async-start(bf16[64,20,1792]{2,1,0:T(8,128)(2,1)} %reshape.97), calls=%async_computation.1 | async-start | bytes 11010048 | tf_op jit(solution)/shard_map/all_to_all | solution.py:57
  384.2 0.0 copy-done.3
  384.2 0.1 copy.13
  384.3 123.8 %all-to-all-done.1 = bf16[64,20,1792]{2,1,0:T(8,128)(2,1)} async-done(((bf16[64,20,1792]{2,1,0:T(8,128)(2,1)}), bf16[64,20,1792]{2,1,0:T(8,128)(2,1)}, u32[]{:S(2)}, u32[]{:S(2)}) %all-to-all-start.1) | async-done | bytes 4587552 | tf_op jit(solution)/shard_map/all_to_all | solution.py:57
  508.1 7.2 %reshape.98 = bf16[1280,1792]{1,0:T(8,128)(2,1)} reshape(bf16[64,20,1792]{2,1,0:T(8,128)(2,1)} %all-to-all-done.1) | data formatting | bytes 9175040 | tf_op jit(solution)/shard_map/reshape | solution.py:58
  515.4 0.0 copy-start.1
  515.4 10.9 %gather_fusion.1 = bf16[1024,1792]{1,0:T(8,128)(2,1)} fusion(bf16[1280,1792]{1,0:T(8,128)(2,1)} %reshape.98, s32[1024]{0:T(1024)S(1)} %broadcast_clamp_fusion), kind=kCustom, calls=%fused_computation.1 | custom fusion | bytes 7344128 | tf_op jit(solution)/shard_map/gather | solution.py:59
  526.3 6.1 %fusion = bf16[128,1792]{1,0:T(8,128)(2,1)} fusion(bf16[1024,1792]{1,0:T(8,128)(2,1)} %gather_fusion.1, f32[128,8]{1,0:T(8,128)S(1)} %copy.13), kind=kLoop, calls=%fused_computation.5 | loop fusion | flops 5275648 | bytes 4132864 | tf_op jit(solution)/shard_map/reduce_sum | solution.py:60
  532.4 0.0 copy-done.1
  (10 shorter events, 0.1 us)
Async XLA Ops:
  6.5 68.2 %copy-start = (bf16[128,1792]{1,0:T(8,128)(2,1)S(1)}, bf16[128,1792]{1,0:T(8,128)(2,1)}, u32[]{:S(2)}) copy-start(bf16[128,1792]{1,0:T(8,128)(2,1)} %param.7) | copy-start | bytes 1376260
  6.5 308.3 %reduce-scatter.4.cloned.1.call-start = ((), (), s32[]{:S(2)}) async-start(), calls=%async_computation.4 | async-start | bytes 6553600
  235.0 8.6 %copy-start.2 = (bf16[1280,1792]{1,0:T(8,128)(2,1)S(1)}, bf16[1280,1792]{1,0:T(8,128)(2,1)}, u32[]{:S(2)}) copy-start(bf16[1280,1792]{1,0:T(8,128)(2,1)} %reshape.96) | copy-start | bytes 13762564
  235.0 8.6 %copy-start.4 = (bf16[1,1792,1024]{2,1,0:T(8,128)(2,1)S(1)}, bf16[1,1792,1024]{2,1,0:T(8,128)(2,1)}, u32[]{:S(2)}) copy-start(bf16[1,1792,1024]{2,1,0:T(8,128)(2,1)} %param.11) | copy-start | bytes 11010052
  259.8 96.2 %all-gather.2.cloned.1.call-start = ((), (), s32[]{:S(2)}) async-start(), calls=%async_computation.3 | async-start | bytes 3276800 | tf_op jit(solution)/shard_map/all_gather | solution.py:52
  373.0 11.1 %copy-start.3 = (f32[128,8]{0,1:T(8,128)S(1)}, f32[128,8]{0,1:T(8,128)}, u32[]{:S(2)}) copy-start(f32[128,8]{0,1:T(8,128)} %param.9) | copy-start | bytes 12292
  373.0 135.1 %all-to-all-start.1 = ((bf16[64,20,1792]{2,1,0:T(8,128)(2,1)}), bf16[64,20,1792]{2,1,0:T(8,128)(2,1)}, u32[]{:S(2)}, u32[]{:S(2)}) async-start(bf16[64,20,1792]{2,1,0:T(8,128)(2,1)} %reshape.97), calls=%async_computation.1 | async-start | bytes 11010048 | tf_op jit(solution)/shard_map/all_to_all | solution.py:57
  515.4 17.0 %copy-start.1 = (bf16[128,1792]{1,0:T(8,128)(2,1)S(1)}, bf16[128,1792]{1,0:T(8,128)(2,1)}, u32[]{:S(2)}) copy-start(bf16[128,1792]{1,0:T(8,128)(2,1)} %param.7) | copy-start | bytes 1376260
Sparse Core Ops, SparseCore 0:
  259.9 54.9 reduce-scatter.3
  318.6 37.3 all-gather.1

commit v2 on v1

v2 whole, which is shorter than its diff:
```python
import jax
import jax.numpy as jnp
from jax import lax
from jax.sharding import PartitionSpec as P


def per_device(tokens, route_ids, route_weights, swap_flags, gate_weight, up_weight, down_weight):
    experts = lax.axis_size("expert")
    tok_rows, quarter = tokens.shape
    choices_per = route_ids.shape[1]
    hidden = gate_weight.shape[2]
    capacity = max(2, min(tok_rows, 5 * tok_rows * choices_per // (4 * experts)))
    w_gate = gate_weight[0]
    w_up = up_weight[0]
    w_down = down_weight[0]
    entries = tok_rows * choices_per
    flat_ids = route_ids.reshape(-1)
    slots = jnp.arange(experts, dtype=jnp.int32)
    onehot = flat_ids[:, None] == slots[None, :]
    entry_ids = jnp.arange(entries, dtype=jnp.int32)
    earlier = (entry_ids[:, None] > entry_ids[None, :]).astype(jnp.bfloat16)
    running = jnp.dot(earlier, onehot.astype(jnp.bfloat16), preferred_element_type=jnp.float32)
    rank_in = jnp.sum(jnp.where(onehot, running, 0.0), axis=1).astype(jnp.int32)
    flag = jnp.sum(jnp.where(onehot, swap_flags[None, :], 0), axis=1)
    home = jnp.where(flag == 1, (flat_ids + experts // 2) % experts, flat_ids)
    slot_of = (home * capacity + rank_in).reshape(tok_rows, choices_per)
    positions = jnp.arange(experts * capacity, dtype=jnp.int32)
    hit = slot_of[:, :, None] == positions[None, None, :]
    pick = jnp.any(hit, axis=1).astype(jnp.bfloat16)
    outgoing = lax.dot_general(
        pick, tokens, (((0,), (0,)), ((), ())), preferred_element_type=jnp.float32
    ).astype(jnp.bfloat16)
    arrived = lax.all_to_all(
        outgoing.reshape(experts, capacity, quarter), "expert", split_axis=0, concat_axis=0, tiled=True
    )
    all_rows = arrived.reshape(experts * capacity, quarter)
    gate_term = jnp.dot(all_rows, w_gate, preferred_element_type=jnp.float32)
    up_term = jnp.dot(all_rows, w_up, preferred_element_type=jnp.float32)
    summed = lax.psum_scatter(
        jnp.concatenate([gate_term, up_term], axis=1).astype(jnp.bfloat16),
        "dp",
        scatter_dimension=0,
        tiled=True,
    ).astype(jnp.float32)
    activated = (jax.nn.silu(summed[:, :hidden]) * summed[:, hidden:]).astype(jnp.bfloat16)
    results = jnp.dot(
        lax.all_gather(activated, "dp", axis=0, tiled=True),
        w_down,
        preferred_element_type=jnp.float32,
    )
    leaving = results.astype(jnp.bfloat16).reshape(experts, capacity, quarter)
    returned = lax.all_to_all(leaving, "expert", split_axis=0, concat_axis=0, tiled=True)
    returned_flat = returned.reshape(experts * capacity, quarter)
    weight_of = jnp.sum(jnp.where(hit, route_weights[:, :, None], 0.0), axis=1)
    weight_hi = weight_of.astype(jnp.bfloat16)
    weight_lo = (weight_of - weight_hi.astype(jnp.float32)).astype(jnp.bfloat16)
    mixed = jnp.dot(weight_hi, returned_flat, preferred_element_type=jnp.float32) + jnp.dot(
        weight_lo, returned_flat, preferred_element_type=jnp.float32
    )
    return mixed.astype(jnp.bfloat16)


def solution(mesh):
    in_specs = (
        P("expert", "dp"),
        P("expert", None),
        P("expert", None),
        P(),
        P("expert", "dp", None),
        P("expert", "dp", None),
        P("expert", None, "dp"),
    )
    out_specs = P("expert", "dp")
    return jax.shard_map(
        per_device, mesh=mesh, in_specs=in_specs, out_specs=out_specs, check_vma=False
    )
```

time: 541 us -> 459 us (0.85)
  other arithmetic: 72.1 us -> 7.43 us
  local copies, waits for them, and re-layouts: 65.2 us -> 41.5 us
  matrix products: 23.9 us -> 32.8 us
    gather x5 -> x0, other arithmetic: 40.6 us -> none  [the longest x3 40.6 us: per_device(): flat_ids = slot_source[route_ids.reshape(-1)]]
    gather x7 -> x0, local copies, waits for them, and re-layouts: 26.8 us -> none  [the longest x2 13 us: per_device(): gathered = tokens[source_tok]]
    another operation x3 -> x0, other arithmetic: 18.2 us -> none
    dot_general x0 -> x4, matrix products: none -> 8.93 us  [the longest x1 3.54 us: per_device(): lax.dot_general(pick, tokens, (((0,), (0,)), ((), ())), preferred_element...]
    reshape x1, local copies, waits for them, and re-layouts: 0.1 us -> 7.21 us  [per_device(): outgoing.reshape(experts, capacity, quarter)]
    unnamed x14 -> x16, local copies, waits for them, and re-layouts: 10.6 us -> 11.1 us
where the time goes in v2:
time: 459 us; the launch traced here: 458 us
  waiting for transfers between devices  215 us (47%)
  blocking collectives  137 us (30%)
  local copies, waits for them, and re-layouts  41.5 us (9%)
  matrix products  32.8 us (7%)
  between operations  13.6 us (3%)
  starting transfers between devices  11.4 us (2%)
  other arithmetic  7.43 us (2%)
    all_to_all x1, blocking collectives, per_device(): lax.all_to_all(outgoing.reshape(experts, capacity, quarter), 'expert', sp...  137 us
    all_to_all x1, waiting for transfers between devices, per_device(): lax.all_to_all(leaving, 'expert', split_axis=0, concat_axis=0, tiled=True)  122 us
    unnamed x3, waiting for transfers between devices  54.8 us
    all_gather x1, waiting for transfers between devices, per_device(): lax.all_gather(activated, 'dp', axis=0, tiled=True)  37.5 us
    unnamed x16, local copies, waits for them, and re-layouts  11.1 us
    all_to_all x1, starting transfers between devices, per_device(): lax.all_to_all(leaving, 'expert', split_axis=0, concat_axis=0, tiled=True)  11.1 us
    dot_general x1, matrix products, per_device(): jnp.dot(lax.all_gather(activated, 'dp', axis=0, tiled=True), w_down, pref...  9.8 us
  transfers between devices with their start and end apart: 3, of which 3 were waited for; matrix products, arithmetic and copies ran while one was open for 0% of the time, Pallas kernels for 0%

profile of v2, /device:TPU:1, one launch (start us, length us, event | category | flops | bytes accessed | tf_op | source)
XLA Modules:
  0.0 458.3 jit_solution(11436442528228465473)
XLA Ops:
  6.5 0.0 copy-start
  6.5 0.0 reduce-scatter.4.cloned.1.call-start
  6.5 0.8 copy.19
  7.4 0.1 eq.41
  7.5 0.6 fusion.8
  8.1 0.1 convert_element_type.37
  8.2 0.8 select_reduce_fusion.1
  9.0 0.1 eq.47
  9.1 1.6 fusion
  10.7 0.0 copy-done
  10.8 3.5 convolution_convert_fusion.1
  14.3 7.2 %reshape.42 = bf16[64,20,1792]{2,1,0:T(8,128)(2,1)} reshape(bf16[1280,1792]{1,0:T(8,128)(2,1)} %convolution_convert_fusion.1) | data formatting | bytes 9175040 | tf_op jit(solution)/shard_map/reshape | solution.py:34
  21.5 137.1 %all_to_all.10 = bf16[64,20,1792]{2,1,0:T(8,128)(2,1)} all-to-all(bf16[64,20,1792]{2,1,0:T(8,128)(2,1)} %reshape.42), channel_id=1, replica_groups=mesh['dp'=4,'expert'=64] {'expert'}, dimensions={0} | all-to-all | bytes 9175040 | tf_op jit(solution)/shard_map/all_to_all | solution.py:33
  158.6 7.2 %reshape.43 = bf16[1280,1792]{1,0:T(8,128)(2,1)} reshape(bf16[64,20,1792]{2,1,0:T(8,128)(2,1)} %all_to_all.10) | data formatting | bytes 9175040 | tf_op jit(solution)/shard_map/reshape | solution.py:36
  165.9 0.0 copy-start.3
  165.9 0.0 copy-start.5
  165.9 8.6 %convolution_convert_fusion.2 = bf16[1280,1024]{0,1:T(8,128)(2,1)S(1)} fusion(bf16[1280,1792]{1,0:T(8,128)(2,1)} %reshape.43, bf16[1,1792,1024]{2,1,0:T(8,128)(2,1)} %param.12), kind=kOutput, calls=%fused_computation.8 | convolution fusion | flops 4698931200 | bytes 10878976 | tf_op jit(solution)/shard_map/dot_general | solution.py:38
  174.4 0.0 copy-done.3
  174.4 0.0 copy-done.5
  174.4 5.5 %convolution_convert_fusion.3 = bf16[1280,1024]{0,1:T(8,128)(2,1)S(1)} fusion(bf16[1280,1792]{1,0:T(8,128)(2,1)S(1)} %copy-done.3, bf16[1,1792,1024]{2,1,0:T(8,128)(2,1)S(1)} %copy-done.5), kind=kOutput, calls=%fused_computation.9 | convolution fusion | flops 4698931200 | bytes 10878976 | tf_op jit(solution)/shard_map/dot_general | solution.py:37
  179.9 2.7 pad_maximum_fusion
  182.6 7.9 %copy.24 = bf16[1280,2048]{1,0:T(8,128)(2,1)} copy(bf16[1280,2048]{0,1:T(8,128)(2,1)} %pad_maximum_fusion) | data formatting | bytes 10485760
  190.5 0.0 reduce-scatter.4.cloned.1.call-update
  190.6 0.3 all-gather.2.cloned.1.call-start
  190.8 54.8 %reduce-scatter.4.cloned.1.call-done = bf16[320,2048]{1,0:T(8,128)(2,1)} async-done(((bf16[1280,2048]{1,0:T(8,128)(2,1)}), bf16[320,2048]{1,0:T(8,128)(2,1)}) %reduce-scatter.4.cloned.1.call-update) | async-done | bytes 1310736
  245.6 1.8 copy.25
  247.5 0.2 convert_element_type.40
  247.7 0.5 fusion.6
  248.2 1.1 copy.23
  249.3 0.0 all-gather.2.cloned.1.call-update
  249.3 37.5 %all-gather.2.cloned.1.call-done = bf16[1280,1024]{1,0:T(8,128)(2,1)} async-done(((bf16[320,1024]{1,0:T(8,128)(2,1)}), bf16[1280,1024]{1,0:T(8,128)(2,1)}) %all-gather.2.cloned.1.call-update) | async-done | bytes 2621456 | tf_op jit(solution)/shard_map/all_gather | solution.py:47
  286.8 9.8 %convolution_convert_fusion = bf16[1280,1792]{1,0:T(8,128)(2,1)} fusion(bf16[1280,1024]{1,0:T(8,128)(2,1)} %all-gather.2.cloned.1.call-done, bf16[1,1024,1792]{2,1,0:T(8,128)(2,1)} %param.13), kind=kOutput, calls=%fused_computation | convolution fusion | flops 4699914240 | bytes 10878976 | tf_op jit(solution)/shard_map/dot_general | solution.py:46
  296.6 7.3 %reshape.44 = bf16[64,20,1792]{2,1,0:T(8,128)(2,1)} reshape(bf16[1280,1792]{1,0:T(8,128)(2,1)} %convolution_convert_fusion) | data formatting | bytes 9175040 | tf_op jit(solution)/shard_map/reshape | solution.py:51
  303.8 0.0 copy-start.4
  303.8 11.1 %all-to-all-start.1 = ((bf16[64,20,1792]{2,1,0:T(8,128)(2,1)}), bf16[64,20,1792]{2,1,0:T(8,128)(2,1)}, u32[]{:S(2)}, u32[]{:S(2)}) async-start(bf16[64,20,1792]{2,1,0:T(8,128)(2,1)} %reshape.44), calls=%async_computation.1 | async-start | bytes 11010048 | tf_op jit(solution)/shard_map/all_to_all | solution.py:52
  315.0 0.0 copy-done.4
  315.0 0.1 copy.22
  315.1 1.6 select_reduce_fusion
  316.7 122.2 %all-to-all-done.1 = bf16[64,20,1792]{2,1,0:T(8,128)(2,1)} async-done(((bf16[64,20,1792]{2,1,0:T(8,128)(2,1)}), bf16[64,20,1792]{2,1,0:T(8,128)(2,1)}, u32[]{:S(2)}, u32[]{:S(2)}) %all-to-all-start.1) | async-done | bytes 4587552 | tf_op jit(solution)/shard_map/all_to_all | solution.py:52
  438.9 7.2 %reshape.45 = bf16[1280,1792]{1,0:T(8,128)(2,1)} reshape(bf16[64,20,1792]{2,1,0:T(8,128)(2,1)} %all-to-all-done.1) | data formatting | bytes 9175040 | tf_op jit(solution)/shard_map/reshape | solution.py:53
  446.2 0.0 copy-start.2
  446.2 0.0 copy-start.1
  446.2 3.2 fusion.10
  449.4 0.4 copy-done.2
  449.9 1.6 fusion.5
  451.4 0.0 copy-done.1
  (3 shorter events, 0.1 us)
Async XLA Ops:
  6.5 4.2 copy-start
  6.5 239.1 %reduce-scatter.4.cloned.1.call-start = ((), (), s32[]{:S(2)}) async-start(), calls=%async_computation.4 | async-start | bytes 6553600
  165.9 8.6 %copy-start.3 = (bf16[1280,1792]{1,0:T(8,128)(2,1)S(1)}, bf16[1280,1792]{1,0:T(8,128)(2,1)}, u32[]{:S(2)}) copy-start(bf16[1280,1792]{1,0:T(8,128)(2,1)} %reshape.43) | copy-start | bytes 13762564
  165.9 8.6 %copy-start.5 = (bf16[1,1792,1024]{2,1,0:T(8,128)(2,1)S(1)}, bf16[1,1792,1024]{2,1,0:T(8,128)(2,1)}, u32[]{:S(2)}) copy-start(bf16[1,1792,1024]{2,1,0:T(8,128)(2,1)} %param.11) | copy-start | bytes 11010052
  190.6 96.2 %all-gather.2.cloned.1.call-start = ((), (), s32[]{:S(2)}) async-start(), calls=%async_computation.3 | async-start | bytes 3276800 | tf_op jit(solution)/shard_map/all_gather | solution.py:47
  303.8 11.1 %copy-start.4 = (f32[128,8]{0,1:T(8,128)S(1)}, f32[128,8]{0,1:T(8,128)}, u32[]{:S(2)}) copy-start(f32[128,8]{0,1:T(8,128)} %param.9) | copy-start | bytes 12292
  303.8 135.1 %all-to-all-start.1 = ((bf16[64,20,1792]{2,1,0:T(8,128)(2,1)}), bf16[64,20,1792]{2,1,0:T(8,128)(2,1)}, u32[]{:S(2)}, u32[]{:S(2)}) async-start(bf16[64,20,1792]{2,1,0:T(8,128)(2,1)} %reshape.44), calls=%async_computation.1 | async-start | bytes 11010048 | tf_op jit(solution)/shard_map/all_to_all | solution.py:52
  446.2 3.7 copy-start.2
  446.2 5.3 %copy-start.1 = (bf16[128,1792]{1,0:T(8,128)(2,1)S(1)}, bf16[128,1792]{1,0:T(8,128)(2,1)}, u32[]{:S(2)}) copy-start(bf16[128,1792]{1,0:T(8,128)(2,1)} %param.7) | copy-start | bytes 1376260
Sparse Core Ops, SparseCore 0:
  190.7 54.9 reduce-scatter.3
  249.4 37.3 all-gather.1

commit v3 on v2

--- a/solution.py
+++ b/solution.py
@@ -30,9 +30,9 @@
     outgoing = lax.dot_general(
         pick, tokens, (((0,), (0,)), ((), ())), preferred_element_type=jnp.float32
     ).astype(jnp.bfloat16)
-    arrived = lax.all_to_all(
-        outgoing.reshape(experts, capacity, quarter), "expert", split_axis=0, concat_axis=0, tiled=True
-    )
+    lane = 128
+    packed = (experts, capacity * quarter // lane, lane)
+    arrived = lax.all_to_all(outgoing.reshape(packed), "expert", split_axis=0, concat_axis=0, tiled=True)
     all_rows = arrived.reshape(experts * capacity, quarter)
     gate_term = jnp.dot(all_rows, w_gate, preferred_element_type=jnp.float32)
     up_term = jnp.dot(all_rows, w_up, preferred_element_type=jnp.float32)
@@ -48,7 +48,7 @@
         w_down,
         preferred_element_type=jnp.float32,
     )
-    leaving = results.astype(jnp.bfloat16).reshape(experts, capacity, quarter)
+    leaving = results.astype(jnp.bfloat16).reshape(packed)
     returned = lax.all_to_all(leaving, "expert", split_axis=0, concat_axis=0, tiled=True)
     returned_flat = returned.reshape(experts * capacity, quarter)
     weight_of = jnp.sum(jnp.where(hit, route_weights[:, :, None], 0.0), axis=1)

time: 459 us -> 430 us (0.937)
  blocking collectives: 137 us -> 117 us
  waiting for transfers between devices: 215 us -> 195 us
  local copies, waits for them, and re-layouts: 41.5 us -> 50.7 us
    all_to_all x1, waiting for transfers between devices: 122 us -> 103 us  [per_device(): lax.all_to_all(leaving, 'expert', split_axis=0, concat_axis=0, tiled=True)]
    all_to_all x1, blocking collectives: 137 us -> 117 us  [per_device(): lax.all_to_all(outgoing.reshape(packed), 'expert', split_axis=0, concat_a...]
    reshape x2, local copies, waits for them, and re-layouts: 14.5 us -> 19.2 us  [the longest x1 9.61 us: per_device(): leaving = results.astype(jnp.bfloat16).reshape(packed)]
where the time goes in v3:
time: 430 us; the launch traced here: 428 us
  waiting for transfers between devices  195 us (45%)
  blocking collectives  117 us (27%)
  local copies, waits for them, and re-layouts  50.7 us (12%)
  matrix products  32.8 us (8%)
  between operations  13.6 us (3%)
  starting transfers between devices  11.4 us (3%)
  other arithmetic  7.43 us (2%)
    all_to_all x1, blocking collectives, per_device(): lax.all_to_all(outgoing.reshape(packed), 'expert', split_axis=0, concat_a...  117 us
    all_to_all x1, waiting for transfers between devices, per_device(): lax.all_to_all(leaving, 'expert', split_axis=0, concat_axis=0, tiled=True)  103 us
    unnamed x3, waiting for transfers between devices  54.9 us
    all_gather x1, waiting for transfers between devices, per_device(): lax.all_gather(activated, 'dp', axis=0, tiled=True)  37.5 us
    unnamed x16, local copies, waits for them, and re-layouts  11.1 us
    all_to_all x1, starting transfers between devices, per_device(): lax.all_to_all(leaving, 'expert', split_axis=0, concat_axis=0, tiled=True)  11.1 us
    dot_general x1, matrix products, per_device(): jnp.dot(lax.all_gather(activated, 'dp', axis=0, tiled=True), w_down, pref...  9.8 us
    reshape x1, local copies, waits for them, and re-layouts, per_device(): leaving = results.astype(jnp.bfloat16).reshape(packed)  9.61 us
  transfers between devices with their start and end apart: 3, of which 3 were waited for; matrix products, arithmetic and copies ran while one was open for 0% of the time, Pallas kernels for 0%

profile of v3, /device:TPU:1, one launch (start us, length us, event | category | flops | bytes accessed | tf_op | source)
XLA Modules:
  0.0 428.3 jit_solution(801983072004560078)
XLA Ops:
  6.5 0.0 copy-start
  6.5 0.0 reduce-scatter.4.cloned.1.call-start
  6.5 0.8 copy.19
  7.4 0.1 eq.41
  7.5 0.6 fusion.8
  8.1 0.1 convert_element_type.37
  8.2 0.8 select_reduce_fusion.1
  9.0 0.1 eq.47
  9.1 1.6 fusion
  10.7 0.0 copy-done
  10.8 3.6 convolution_convert_fusion.1
  14.3 9.6 %reshape.42 = bf16[64,280,128]{2,1,0:T(8,128)(2,1)} reshape(bf16[1280,1792]{1,0:T(8,128)(2,1)} %convolution_convert_fusion.1) | data formatting | bytes 9175040 | tf_op jit(solution)/shard_map/reshape | solution.py:35
  23.9 117.5 %all_to_all.10 = bf16[64,280,128]{2,1,0:T(8,128)(2,1)} all-to-all(bf16[64,280,128]{2,1,0:T(8,128)(2,1)} %reshape.42), channel_id=1, replica_groups=mesh['dp'=4,'expert'=64] {'expert'}, dimensions={0} | all-to-all | bytes 9175040 | tf_op jit(solution)/shard_map/all_to_all | solution.py:35
  141.4 9.5 %reshape.43 = bf16[1280,1792]{1,0:T(8,128)(2,1)} reshape(bf16[64,280,128]{2,1,0:T(8,128)(2,1)} %all_to_all.10) | data formatting | bytes 9175040 | tf_op jit(solution)/shard_map/reshape | solution.py:36
  150.9 0.0 copy-start.3
  150.9 0.0 copy-start.5
  150.9 8.6 %convolution_convert_fusion.2 = bf16[1280,1024]{0,1:T(8,128)(2,1)S(1)} fusion(bf16[1280,1792]{1,0:T(8,128)(2,1)} %reshape.43, bf16[1,1792,1024]{2,1,0:T(8,128)(2,1)} %param.12), kind=kOutput, calls=%fused_computation.8 | convolution fusion | flops 4698931200 | bytes 10878976 | tf_op jit(solution)/shard_map/dot_general | solution.py:38
  159.5 0.0 copy-done.3
  159.5 0.0 copy-done.5
  159.5 5.5 %convolution_convert_fusion.3 = bf16[1280,1024]{0,1:T(8,128)(2,1)S(1)} fusion(bf16[1280,1792]{1,0:T(8,128)(2,1)S(1)} %copy-done.3, bf16[1,1792,1024]{2,1,0:T(8,128)(2,1)S(1)} %copy-done.5), kind=kOutput, calls=%fused_computation.9 | convolution fusion | flops 4698931200 | bytes 10878976 | tf_op jit(solution)/shard_map/dot_general | solution.py:37
  165.0 2.7 pad_maximum_fusion
  167.7 7.9 %copy.24 = bf16[1280,2048]{1,0:T(8,128)(2,1)} copy(bf16[1280,2048]{0,1:T(8,128)(2,1)} %pad_maximum_fusion) | data formatting | bytes 10485760
  175.6 0.0 reduce-scatter.4.cloned.1.call-update
  175.6 0.3 all-gather.2.cloned.1.call-start
  175.9 54.9 %reduce-scatter.4.cloned.1.call-done = bf16[320,2048]{1,0:T(8,128)(2,1)} async-done(((bf16[1280,2048]{1,0:T(8,128)(2,1)}), bf16[320,2048]{1,0:T(8,128)(2,1)}) %reduce-scatter.4.cloned.1.call-update) | async-done | bytes 1310736
  230.8 1.8 copy.25
  232.6 0.2 convert_element_type.40
  232.8 0.5 fusion.6
  233.3 1.1 copy.23
  234.4 0.0 all-gather.2.cloned.1.call-update
  234.4 37.5 %all-gather.2.cloned.1.call-done = bf16[1280,1024]{1,0:T(8,128)(2,1)} async-done(((bf16[320,1024]{1,0:T(8,128)(2,1)}), bf16[1280,1024]{1,0:T(8,128)(2,1)}) %all-gather.2.cloned.1.call-update) | async-done | bytes 2621456 | tf_op jit(solution)/shard_map/all_gather | solution.py:47
  271.9 9.8 %convolution_convert_fusion = bf16[1280,1792]{1,0:T(8,128)(2,1)} fusion(bf16[1280,1024]{1,0:T(8,128)(2,1)} %all-gather.2.cloned.1.call-done, bf16[1,1024,1792]{2,1,0:T(8,128)(2,1)} %param.13), kind=kOutput, calls=%fused_computation | convolution fusion | flops 4699914240 | bytes 10878976 | tf_op jit(solution)/shard_map/dot_general | solution.py:46
  281.7 9.6 %reshape.44 = bf16[64,280,128]{2,1,0:T(8,128)(2,1)} reshape(bf16[1280,1792]{1,0:T(8,128)(2,1)} %convolution_convert_fusion) | data formatting | bytes 9175040 | tf_op jit(solution)/shard_map/reshape | solution.py:51
  291.3 0.0 copy-start.4
  291.3 11.1 %all-to-all-start.1 = ((bf16[64,280,128]{2,1,0:T(8,128)(2,1)}), bf16[64,280,128]{2,1,0:T(8,128)(2,1)}, u32[]{:S(2)}, u32[]{:S(2)}) async-start(bf16[64,280,128]{2,1,0:T(8,128)(2,1)} %reshape.44), calls=%async_computation.1 | async-start | bytes 9175040 | tf_op jit(solution)/shard_map/all_to_all | solution.py:52
  302.4 0.0 copy-done.4
  302.5 0.1 copy.22
  302.6 1.6 select_reduce_fusion
  304.2 102.6 %all-to-all-done.1 = bf16[64,280,128]{2,1,0:T(8,128)(2,1)} async-done(((bf16[64,280,128]{2,1,0:T(8,128)(2,1)}), bf16[64,280,128]{2,1,0:T(8,128)(2,1)}, u32[]{:S(2)}, u32[]{:S(2)}) %all-to-all-start.1) | async-done | bytes 4587552 | tf_op jit(solution)/shard_map/all_to_all | solution.py:52
  406.7 9.5 %reshape.45 = bf16[1280,1792]{1,0:T(8,128)(2,1)} reshape(bf16[64,280,128]{2,1,0:T(8,128)(2,1)} %all-to-all-done.1) | data formatting | bytes 9175040 | tf_op jit(solution)/shard_map/reshape | solution.py:53
  416.2 0.0 copy-start.2
  416.2 0.0 copy-start.1
  416.2 3.2 fusion.10
  419.5 0.4 copy-done.2
  419.9 1.6 fusion.5
  421.5 0.0 copy-done.1
  (3 shorter events, 0.1 us)
Async XLA Ops:
  6.5 4.2 copy-start
  6.5 224.2 %reduce-scatter.4.cloned.1.call-start = ((), (), s32[]{:S(2)}) async-start(), calls=%async_computation.4 | async-start | bytes 6553600
  150.9 8.6 %copy-start.3 = (bf16[1280,1792]{1,0:T(8,128)(2,1)S(1)}, bf16[1280,1792]{1,0:T(8,128)(2,1)}, u32[]{:S(2)}) copy-start(bf16[1280,1792]{1,0:T(8,128)(2,1)} %reshape.43) | copy-start | bytes 13762564
  150.9 8.6 %copy-start.5 = (bf16[1,1792,1024]{2,1,0:T(8,128)(2,1)S(1)}, bf16[1,1792,1024]{2,1,0:T(8,128)(2,1)}, u32[]{:S(2)}) copy-start(bf16[1,1792,1024]{2,1,0:T(8,128)(2,1)} %param.11) | copy-start | bytes 11010052
  175.6 96.3 %all-gather.2.cloned.1.call-start = ((), (), s32[]{:S(2)}) async-start(), calls=%async_computation.3 | async-start | bytes 3276800 | tf_op jit(solution)/shard_map/all_gather | solution.py:47
  291.3 11.1 %copy-start.4 = (f32[128,8]{0,1:T(8,128)S(1)}, f32[128,8]{0,1:T(8,128)}, u32[]{:S(2)}) copy-start(f32[128,8]{0,1:T(8,128)} %param.9) | copy-start | bytes 12292
  291.3 115.4 %all-to-all-start.1 = ((bf16[64,280,128]{2,1,0:T(8,128)(2,1)}), bf16[64,280,128]{2,1,0:T(8,128)(2,1)}, u32[]{:S(2)}, u32[]{:S(2)}) async-start(bf16[64,280,128]{2,1,0:T(8,128)(2,1)} %reshape.44), calls=%async_computation.1 | async-start | bytes 9175040 | tf_op jit(solution)/shard_map/all_to_all | solution.py:52
  416.2 3.7 copy-start.2
  416.2 5.3 %copy-start.1 = (bf16[128,1792]{1,0:T(8,128)(2,1)S(1)}, bf16[128,1792]{1,0:T(8,128)(2,1)}, u32[]{:S(2)}) copy-start(bf16[128,1792]{1,0:T(8,128)(2,1)} %param.7) | copy-start | bytes 1376260
Sparse Core Ops, SparseCore 0:
  175.7 54.9 reduce-scatter.3
  234.5 37.3 all-gather.1

commit v4 on v3

v4 whole, which is shorter than its diff:
```python
import jax
import jax.numpy as jnp
from jax import lax
from jax.sharding import PartitionSpec as P


def expert_rows(rows, w_gate, w_up, w_down, hidden):
    gate_term = jnp.dot(rows, w_gate, preferred_element_type=jnp.float32)
    up_term = jnp.dot(rows, w_up, preferred_element_type=jnp.float32)
    summed = lax.psum_scatter(
        jnp.concatenate([gate_term, up_term], axis=1).astype(jnp.bfloat16),
        "dp",
        scatter_dimension=0,
        tiled=True,
    ).astype(jnp.float32)
    activated = (jax.nn.silu(summed[:, :hidden]) * summed[:, hidden:]).astype(jnp.bfloat16)
    results = jnp.dot(
        lax.all_gather(activated, "dp", axis=0, tiled=True),
        w_down,
        preferred_element_type=jnp.float32,
    )
    return results.astype(jnp.bfloat16)


def per_device(tokens, route_ids, route_weights, swap_flags, gate_weight, up_weight, down_weight):
    experts = lax.axis_size("expert")
    tok_rows, quarter = tokens.shape
    choices_per = route_ids.shape[1]
    hidden = gate_weight.shape[2]
    capacity = max(2, min(tok_rows, 5 * tok_rows * choices_per // (4 * experts)))
    w_gate = gate_weight[0]
    w_up = up_weight[0]
    w_down = down_weight[0]
    entries = tok_rows * choices_per
    flat_ids = route_ids.reshape(-1)
    slots = jnp.arange(experts, dtype=jnp.int32)
    onehot = flat_ids[:, None] == slots[None, :]
    entry_ids = jnp.arange(entries, dtype=jnp.int32)
    earlier = (entry_ids[:, None] > entry_ids[None, :]).astype(jnp.bfloat16)
    running = jnp.dot(earlier, onehot.astype(jnp.bfloat16), preferred_element_type=jnp.float32)
    rank_in = jnp.sum(jnp.where(onehot, running, 0.0), axis=1).astype(jnp.int32)
    flag = jnp.sum(jnp.where(onehot, swap_flags[None, :], 0), axis=1)
    home = jnp.where(flag == 1, (flat_ids + experts // 2) % experts, flat_ids)
    home = home.reshape(tok_rows, choices_per)
    rank_in = rank_in.reshape(tok_rows, choices_per)
    pieces = 2 if capacity % 2 == 0 else 1
    share = capacity // pieces
    lane = 128
    packed = (experts, share * quarter // lane, lane)
    positions = jnp.arange(experts * share, dtype=jnp.int32)
    mixed = jnp.zeros((tok_rows, quarter), jnp.float32)
    for piece in range(pieces):
        inside = (rank_in >= piece * share) & (rank_in < (piece + 1) * share)
        slot_of = jnp.where(inside, home * share + rank_in - piece * share, -1)
        hit = slot_of[:, :, None] == positions[None, None, :]
        pick = jnp.any(hit, axis=1).astype(jnp.bfloat16)
        outgoing = lax.dot_general(
            pick, tokens, (((0,), (0,)), ((), ())), preferred_element_type=jnp.float32
        ).astype(jnp.bfloat16)
        arrived = lax.all_to_all(outgoing.reshape(packed), "expert", split_axis=0, concat_axis=0, tiled=True)
        served = expert_rows(arrived.reshape(experts * share, quarter), w_gate, w_up, w_down, hidden)
        returned = lax.all_to_all(served.reshape(packed), "expert", split_axis=0, concat_axis=0, tiled=True)
        returned_flat = returned.reshape(experts * share, quarter)
        weight_of = jnp.sum(jnp.where(hit, route_weights[:, :, None], 0.0), axis=1)
        weight_hi = weight_of.astype(jnp.bfloat16)
        weight_lo = (weight_of - weight_hi.astype(jnp.float32)).astype(jnp.bfloat16)
        mixed = mixed + jnp.dot(weight_hi, returned_flat, preferred_element_type=jnp.float32)
        mixed = mixed + jnp.dot(weight_lo, returned_flat, preferred_element_type=jnp.float32)
    return mixed.astype(jnp.bfloat16)


def solution(mesh):
    in_specs = (
        P("expert", "dp"),
        P("expert", None),
        P("expert", None),
        P(),
        P("expert", "dp", None),
        P("expert", "dp", None),
        P("expert", None, "dp"),
    )
    out_specs = P("expert", "dp")
    return jax.shard_map(
        per_device, mesh=mesh, in_specs=in_specs, out_specs=out_specs, check_vma=False
    )
```

time: 430 us -> 339 us (0.79)
  waiting for transfers between devices: 195 us -> 147 us
  blocking collectives: 117 us -> 69.8 us
  local copies, waits for them, and re-layouts: 50.7 us -> 35.8 us
  starting transfers between devices: 11.4 us -> 24.2 us
  other arithmetic: 7.43 us -> 12.6 us
    unnamed x3 -> x4, waiting for transfers between devices: 54.9 us -> 0.07 us
    all_to_all x1, blocking collectives: 117 us -> 69.8 us  [per_device(): lax.all_to_all(outgoing.reshape(packed), 'expert', split_axis=0, concat_a...]
    reduce_scatter x0 -> x2, waiting for transfers between devices: none -> 41.5 us  [expert_rows(): lax.psum_scatter(jnp.concatenate([gate_term, up_term], axis=1).astype(jnp...]
    all_to_all x1 -> x3, waiting for transfers between devices: 103 us -> 79.3 us  [the longest x2 48 us: per_device(): lax.all_to_all(served.reshape(packed), 'expert', split_axis=0, concat_axi...]
    all_to_all x1 -> x3, starting transfers between devices: 11.1 us -> 23.9 us  [the longest x2 17.9 us: per_device(): lax.all_to_all(served.reshape(packed), 'expert', split_axis=0, concat_axi...]
    all_gather x1 -> x2, waiting for transfers between devices: 37.5 us -> 26.2 us  [expert_rows(): lax.all_gather(activated, 'dp', axis=0, tiled=True)]
    unnamed x16, local copies, waits for them, and re-layouts: 11.1 us -> 2.41 us
    reshape x3 -> x6, local copies, waits for them, and re-layouts: 28.6 us -> 25.1 us  [the longest x2 9.11 us: per_device(): served.reshape(packed)]
  transfers between devices with their start and end apart: 3 -> 7, of which waited for: 3 -> 5; matrix products, arithmetic and copies ran while one was open for 0% -> 15% of each run, Pallas kernels for 0% -> 0%
where the time goes in v4:
time: 339 us; the launch traced here: 338 us
  waiting for transfers between devices  147 us (43%)
  blocking collectives  69.8 us (21%)
  local copies, waits for them, and re-layouts  35.8 us (11%)
  matrix products  35.3 us (10%)
  starting transfers between devices  24.2 us (7%)
  between operations  13.4 us (4%)
  other arithmetic  12.6 us (4%)
    all_to_all x1, blocking collectives, per_device(): lax.all_to_all(outgoing.reshape(packed), 'expert', split_axis=0, concat_a...  69.8 us
    all_to_all x2, waiting for transfers between devices, per_device(): lax.all_to_all(served.reshape(packed), 'expert', split_axis=0, concat_axi...  48 us
    reduce_scatter x2, waiting for transfers between devices, expert_rows(): lax.psum_scatter(jnp.concatenate([gate_term, up_term], axis=1).astype(jnp...  41.5 us
    all_to_all x1, waiting for transfers between devices, per_device(): lax.all_to_all(outgoing.reshape(packed), 'expert', split_axis=0, concat_a...  31.3 us
    all_gather x2, waiting for transfers between devices, expert_rows(): lax.all_gather(activated, 'dp', axis=0, tiled=True)  26.2 us
    all_to_all x2, starting transfers between devices, per_device(): lax.all_to_all(served.reshape(packed), 'expert', split_axis=0, concat_axi...  17.9 us
    dot_general x2, matrix products, expert_rows(): jnp.dot(lax.all_gather(activated, 'dp', axis=0, tiled=True), w_down, pref...  11.4 us
    dot_general x2, matrix products, expert_rows(): gate_term = jnp.dot(rows, w_gate, preferred_element_type=jnp.float32)  10.1 us
  transfers between devices with their start and end apart: 7, of which 5 were waited for; matrix products, arithmetic and copies ran while one was open for 15% of the time, Pallas kernels for 0%

profile of v4, /device:TPU:1, one launch (start us, length us, event | category | flops | bytes accessed | tf_op | source)
XLA Modules:
  0.0 338.1 jit_solution(14122640178325459012)
XLA Ops:
  6.5 0.0 copy-start
  6.5 0.0 reduce-scatter.3.cloned.1.call-start
  6.5 0.8 copy.15
  7.4 0.1 eq.53
  7.5 0.6 fusion.35
  8.1 0.1 convert_element_type.59
  8.2 0.8 select_reduce_fusion.2
  9.0 0.1 eq.59
  9.1 0.1 add_select_fusion.1
  9.1 1.8 fusion.19
  10.9 0.0 copy-done
  10.9 2.2 convolution_convert_fusion.1
  13.1 4.3 %reshape.37 = bf16[64,140,128]{2,1,0:T(8,128)(2,1)S(1)} reshape(bf16[640,1792]{1,0:T(8,128)(2,1)} %convolution_convert_fusion.1) | data formatting | bytes 4587520 | tf_op jit(solution)/shard_map/reshape | solution.py:60
  17.4 69.8 %all_to_all.20 = bf16[64,140,128]{2,1,0:T(8,128)(2,1)} all-to-all(bf16[64,140,128]{2,1,0:T(8,128)(2,1)S(1)} %reshape.37), channel_id=1, replica_groups=mesh['dp'=4,'expert'=64] {'expert'}, dimensions={0} | all-to-all | bytes 4587520 | tf_op jit(solution)/shard_map/all_to_all | solution.py:60
  87.2 4.1 %reshape.38 = bf16[640,1792]{1,0:T(8,128)(2,1)S(1)} reshape(bf16[64,140,128]{2,1,0:T(8,128)(2,1)} %all_to_all.20) | data formatting | bytes 4587520 | tf_op jit(solution)/shard_map/reshape | solution.py:61
  91.3 0.0 copy-start.5
  91.3 4.7 %fusion.22 = bf16[640,1024]{1,0:T(8,128)(2,1)S(1)} fusion(bf16[640,1792]{1,0:T(8,128)(2,1)S(1)} %reshape.38, bf16[1,1792,1024]{2,1,0:T(8,128)(2,1)} %param.11), kind=kOutput, calls=%fused_computation.30 | convolution fusion | flops 2349465600 | bytes 7274496 | tf_op jit(solution)/shard_map/dot_general | solution.py:8
  96.1 0.0 copy-done.5
  96.1 2.6 fusion.28
  98.7 1.7 pad_maximum_fusion
  100.4 0.0 reduce-scatter.3.cloned.1.call-update
  100.4 0.8 convolution_convert_fusion
  101.2 3.7 %reshape.41 = bf16[64,140,128]{2,1,0:T(8,128)(2,1)} reshape(bf16[640,1792]{1,0:T(8,128)(2,1)S(1)} %convolution_convert_fusion) | data formatting | bytes 4587520 | tf_op jit(solution)/shard_map/reshape | solution.py:60
  105.0 6.0 %all-to-all-start.2 = ((bf16[64,140,128]{2,1,0:T(8,128)(2,1)}), bf16[64,140,128]{2,1,0:T(8,128)(2,1)S(1)}, u32[]{:S(2)}, u32[]{:S(2)}) async-start(bf16[64,140,128]{2,1,0:T(8,128)(2,1)} %reshape.41), calls=%async_computation.3 | async-start | bytes 4718592 | tf_op jit(solution)/shard_map/all_to_all | solution.py:60
  111.0 0.0 all-gather.3.cloned.1.call-start
  111.1 22.9 %reduce-scatter.3.cloned.1.call-done = bf16[160,2048]{1,0:T(8,128)(2,1)} async-done(((bf16[640,2048]{1,0:T(8,128)(2,1)}), bf16[160,2048]{1,0:T(8,128)(2,1)}) %reduce-scatter.3.cloned.1.call-update) | async-done | bytes 655376 | tf_op jit(solution)/shard_map/reduce_scatter | solution.py:10
  133.9 1.2 convert_element_type.62
  135.2 0.9 fusion.37
  136.1 0.0 all-gather.3.cloned.1.call-update
  136.1 0.2 reduce-scatter.5.cloned.1.call-start
  136.3 31.3 %all-to-all-done.2 = bf16[64,140,128]{2,1,0:T(8,128)(2,1)S(1)} async-done(((bf16[64,140,128]{2,1,0:T(8,128)(2,1)}), bf16[64,140,128]{2,1,0:T(8,128)(2,1)S(1)}, u32[]{:S(2)}, u32[]{:S(2)}) %all-to-all-start.2) | async-done | bytes 2293792 | tf_op jit(solution)/shard_map/all_to_all | solution.py:60
  167.6 3.6 %reshape.42 = bf16[640,1792]{1,0:T(8,128)(2,1)} reshape(bf16[64,140,128]{2,1,0:T(8,128)(2,1)S(1)} %all-to-all-done.2) | data formatting | bytes 4587520 | tf_op jit(solution)/shard_map/reshape | solution.py:61
  171.2 5.4 %fusion.25 = bf16[640,1024]{1,0:T(8,128)(2,1)S(1)} fusion(bf16[640,1792]{1,0:T(8,128)(2,1)} %reshape.42, bf16[1,1792,1024]{2,1,0:T(8,128)(2,1)} %param.11), kind=kOutput, calls=%fused_computation.31 | convolution fusion | flops 2349465600 | bytes 7274496 | tf_op jit(solution)/shard_map/dot_general | solution.py:8
  176.6 0.0 copy-done.3
  176.6 0.0 copy-done.6
  176.6 2.5 fusion.31
  179.2 1.7 pad_maximum_fusion.1
  180.9 0.0 reduce-scatter.5.cloned.1.call-update
  181.0 0.0 all-gather.3.cloned.1.call-done
  181.0 5.0 %fusion.13 = bf16[640,1792]{1,0:T(8,128)(2,1)S(1)} fusion(bf16[640,1024]{1,0:T(8,128)(2,1)} %all-gather.3.cloned.1.call-done, bf16[1,1024,1792]{2,1,0:T(8,128)(2,1)} %param.13), kind=kOutput, calls=%fused_computation.14 | convolution fusion | flops 2349957120 | bytes 7274496 | tf_op jit(solution)/shard_map/dot_general | solution.py:17
  186.0 3.8 %reshape.39 = bf16[64,140,128]{2,1,0:T(8,128)(2,1)} reshape(bf16[640,1792]{1,0:T(8,128)(2,1)S(1)} %fusion.13) | data formatting | bytes 4587520 | tf_op jit(solution)/shard_map/reshape | solution.py:62
  189.7 5.9 %all-to-all-start.1 = ((bf16[64,140,128]{2,1,0:T(8,128)(2,1)}), bf16[64,140,128]{2,1,0:T(8,128)(2,1)S(1)}, u32[]{:S(2)}, u32[]{:S(2)}) async-start(bf16[64,140,128]{2,1,0:T(8,128)(2,1)} %reshape.39), calls=%async_computation.2 | async-start | bytes 4718592 | tf_op jit(solution)/shard_map/all_to_all | solution.py:62
  195.7 0.0 all-gather.5.cloned.1.call-start
  195.8 18.6 %reduce-scatter.5.cloned.1.call-done = bf16[160,2048]{1,0:T(8,128)(2,1)} async-done(((bf16[640,2048]{1,0:T(8,128)(2,1)}), bf16[160,2048]{1,0:T(8,128)(2,1)}) %reduce-scatter.5.cloned.1.call-update) | async-done | bytes 655376 | tf_op jit(solution)/shard_map/reduce_scatter | solution.py:10
  214.4 1.2 convert_element_type.69
  215.6 0.9 fusion.36
  216.5 0.0 all-gather.5.cloned.1.call-update
  216.5 26.2 %all-gather.5.cloned.1.call-done = bf16[640,1024]{1,0:T(8,128)(2,1)} async-done(((bf16[160,1024]{1,0:T(8,128)(2,1)}), bf16[640,1024]{1,0:T(8,128)(2,1)}) %all-gather.5.cloned.1.call-update) | async-done | bytes 1310736 | tf_op jit(solution)/shard_map/all_gather | solution.py:18
  242.7 6.4 %fusion.16 = bf16[640,1792]{1,0:T(8,128)(2,1)} fusion(bf16[640,1024]{1,0:T(8,128)(2,1)} %all-gather.5.cloned.1.call-done, bf16[1,1024,1792]{2,1,0:T(8,128)(2,1)} %param.13), kind=kOutput, calls=%fused_computation.15 | convolution fusion | flops 2349957120 | bytes 7274496 | tf_op jit(solution)/shard_map/dot_general | solution.py:17
  249.1 5.3 %reshape.43 = bf16[64,140,128]{2,1,0:T(8,128)(2,1)} reshape(bf16[640,1792]{1,0:T(8,128)(2,1)} %fusion.16) | data formatting | bytes 4587520 | tf_op jit(solution)/shard_map/reshape | solution.py:62
  254.5 0.0 all-to-all-done.1
  254.5 1.4 copy-done.2
  255.9 11.9 %all-to-all-start.3 = ((bf16[64,140,128]{2,1,0:T(8,128)(2,1)}), bf16[64,140,128]{2,1,0:T(8,128)(2,1)}, u32[]{:S(2)}, u32[]{:S(2)}) async-start(bf16[64,140,128]{2,1,0:T(8,128)(2,1)} %reshape.43), calls=%async_computation.5 | async-start | bytes 4718592 | tf_op jit(solution)/shard_map/all_to_all | solution.py:62
  267.8 0.0 copy-done.4
  267.8 0.1 copy.18
  267.9 2.2 select_reduce_fusion
  270.2 4.1 %reshape.40 = bf16[640,1792]{1,0:T(8,128)(2,1)S(1)} reshape(bf16[64,140,128]{2,1,0:T(8,128)(2,1)} %copy-done.2) | data formatting | bytes 4587520 | tf_op jit(solution)/shard_map/reshape | solution.py:63
  274.3 0.5 fusion.42
  274.8 1.5 convolution_add_fusion.2
  276.4 48.0 %all-to-all-done.3 = bf16[64,140,128]{2,1,0:T(8,128)(2,1)} async-done(((bf16[64,140,128]{2,1,0:T(8,128)(2,1)}), bf16[64,140,128]{2,1,0:T(8,128)(2,1)}, u32[]{:S(2)}, u32[]{:S(2)}) %all-to-all-start.3) | async-done | bytes 2293792 | tf_op jit(solution)/shard_map/all_to_all | solution.py:62
  324.4 4.1 %reshape.44 = bf16[640,1792]{1,0:T(8,128)(2,1)S(1)} reshape(bf16[64,140,128]{2,1,0:T(8,128)(2,1)} %all-to-all-done.3) | data formatting | bytes 4587520 | tf_op jit(solution)/shard_map/reshape | solution.py:63
  328.5 0.0 copy-start.1
  328.5 1.8 convolution_add_fusion.1
  330.3 1.3 fusion.21
  (7 shorter events, 0.0 us)
Async XLA Ops:
  6.5 4.4 %copy-start = (bf16[128,1792]{1,0:T(8,128)(2,1)S(1)}, bf16[128,1792]{1,0:T(8,128)(2,1)}, u32[]{:S(2)}) copy-start(bf16[128,1792]{1,0:T(8,128)(2,1)} %param.7) | copy-start | bytes 1376260
  6.5 127.4 %reduce-scatter.3.cloned.1.call-start = ((), (), s32[]{:S(2)}) async-start(), calls=%async_computation.6 | async-start | bytes 3276800 | tf_op jit(solution)/shard_map/reduce_scatter | solution.py:10
  91.3 4.7 %copy-start.5 = (bf16[1,1792,1024]{2,1,0:T(8,128)(2,1)S(1)}, bf16[1,1792,1024]{2,1,0:T(8,128)(2,1)}, u32[]{:S(2)}) copy-start(bf16[1,1792,1024]{2,1,0:T(8,128)(2,1)} %param.12) | copy-start | bytes 11010052
  105.0 62.7 %all-to-all-start.2 = ((bf16[64,140,128]{2,1,0:T(8,128)(2,1)}), bf16[64,140,128]{2,1,0:T(8,128)(2,1)S(1)}, u32[]{:S(2)}, u32[]{:S(2)}) async-start(bf16[64,140,128]{2,1,0:T(8,128)(2,1)} %reshape.41), calls=%async_computation.3 | async-start | bytes 4718592 | tf_op jit(solution)/shard_map/all_to_all | solution.py:60
  111.0 69.9 %all-gather.3.cloned.1.call-start = ((), (), s32[]{:S(2)}) async-start(), calls=%async_computation.7 | async-start | bytes 1638400 | tf_op jit(solution)/shard_map/all_gather | solution.py:18
  136.1 78.3 %reduce-scatter.5.cloned.1.call-start = ((), (), s32[]{:S(2)}) async-start(), calls=%async_computation.8 | async-start | bytes 3276800 | tf_op jit(solution)/shard_map/reduce_scatter | solution.py:10
  171.2 5.4 %copy-start.3 = (bf16[640,1792]{1,0:T(8,128)(2,1)S(1)}, bf16[640,1792]{1,0:T(8,128)(2,1)}, u32[]{:S(2)}) copy-start(bf16[640,1792]{1,0:T(8,128)(2,1)} %reshape.42) | copy-start | bytes 6881284
  171.2 5.4 %copy-start.6 = (bf16[1,1792,1024]{2,1,0:T(8,128)(2,1)S(1)}, bf16[1,1792,1024]{2,1,0:T(8,128)(2,1)}, u32[]{:S(2)}) copy-start(bf16[1,1792,1024]{2,1,0:T(8,128)(2,1)} %param.12) | copy-start | bytes 11010052
  189.7 64.7 %all-to-all-start.1 = ((bf16[64,140,128]{2,1,0:T(8,128)(2,1)}), bf16[64,140,128]{2,1,0:T(8,128)(2,1)S(1)}, u32[]{:S(2)}, u32[]{:S(2)}) async-start(bf16[64,140,128]{2,1,0:T(8,128)(2,1)} %reshape.39), calls=%async_computation.2 | async-start | bytes 4718592 | tf_op jit(solution)/shard_map/all_to_all | solution.py:62
  195.7 47.0 %all-gather.5.cloned.1.call-start = ((), (), s32[]{:S(2)}) async-start(), calls=%async_computation.9 | async-start | bytes 1638400 | tf_op jit(solution)/shard_map/all_gather | solution.py:18
  254.5 13.4 %copy-start.4 = (f32[128,8]{0,1:T(8,128)S(1)}, f32[128,8]{0,1:T(8,128)}, u32[]{:S(2)}) copy-start(f32[128,8]{0,1:T(8,128)} %param.9) | copy-start | bytes 12292
  254.5 1.4 copy-start.2
  255.9 68.5 %all-to-all-start.3 = ((bf16[64,140,128]{2,1,0:T(8,128)(2,1)}), bf16[64,140,128]{2,1,0:T(8,128)(2,1)}, u32[]{:S(2)}, u32[]{:S(2)}) async-start(bf16[64,140,128]{2,1,0:T(8,128)(2,1)} %reshape.43), calls=%async_computation.5 | async-start | bytes 4718592 | tf_op jit(solution)/shard_map/all_to_all | solution.py:62
  328.5 3.1 copy-start.1
Sparse Core Ops, SparseCore 0:
  100.5 33.3 reduce-scatter.2
  136.2 26.0 all-gather.2
  181.1 33.2 reduce-scatter.4
  216.7 26.0 all-gather.4

commit v5 on v4

--- a/solution.py
+++ b/solution.py
@@ -3,12 +3,39 @@
 from jax import lax
 from jax.sharding import PartitionSpec as P
 
+from jax.experimental import pallas as pl
+
+
+def gate_up_kernel(x_ref, wg_ref, wu_ref, o_ref):
+    col = pl.program_id(0)
+    width = wg_ref.shape[1]
+    half = width * pl.num_programs(0)
+    x = x_ref[...]
+    gate = jnp.dot(x, wg_ref[...], preferred_element_type=jnp.float32)
+    up = jnp.dot(x, wu_ref[...], preferred_element_type=jnp.float32)
+    o_ref[:, pl.ds(pl.multiple_of(col * width, width), width)] = gate.astype(o_ref.dtype)
+    o_ref[:, pl.ds(pl.multiple_of(half + col * width, width), width)] = up.astype(o_ref.dtype)
+
+
+def gate_up(x, wg, wu, width=256):
+    rows, depth = x.shape
+    hidden = wg.shape[1]
+    return pl.pallas_call(
+        gate_up_kernel,
+        grid=(hidden // width,),
+        in_specs=[
+            pl.BlockSpec((rows, depth), lambda c: (0, 0)),
+            pl.BlockSpec((depth, width), lambda c: (0, c)),
+            pl.BlockSpec((depth, width), lambda c: (0, c)),
+        ],
+        out_specs=pl.BlockSpec((rows, 2 * hidden), lambda c: (0, 0)),
+        out_shape=jax.ShapeDtypeStruct((rows, 2 * hidden), jnp.bfloat16),
+    )(x, wg, wu)
+
 
 def expert_rows(rows, w_gate, w_up, w_down, hidden):
-    gate_term = jnp.dot(rows, w_gate, preferred_element_type=jnp.float32)
-    up_term = jnp.dot(rows, w_up, preferred_element_type=jnp.float32)
     summed = lax.psum_scatter(
-        jnp.concatenate([gate_term, up_term], axis=1).astype(jnp.bfloat16),
+        gate_up(rows, w_gate, w_up),
         "dp",
         scatter_dimension=0,
         tiled=True,

time: 339 us -> 340 us (level)
  Pallas kernels: 0 us -> 18.9 us
  matrix products: 35.3 us -> 20 us
  other arithmetic: 12.6 us -> 9.1 us
    pallas_call x0 -> x2, Pallas kernels: none -> 18.9 us  [gate_up(): pl.pallas_call(gate_up_kernel, grid=(hidden // width,), in_specs=[pl.Bloc...]
    dot_general x4 -> x0, matrix products: 15.2 us -> none  [the longest x2 10.1 us: expert_rows(): gate_term = jnp.dot(rows, w_gate, preferred_element_type=jnp.float32)]
    concatenate x2 -> x0, other arithmetic: 3.48 us -> none  [expert_rows(): jnp.concatenate([gate_term, up_term], axis=1).astype(jnp.bfloat16)]
  transfers between devices with their start and end apart: 7 -> 7, of which waited for: 5 -> 5; matrix products, arithmetic and copies ran while one was open for 15% -> 12% of each run, Pallas kernels for 0% -> 3%
where the time goes in v5:
time: 340 us; the launch traced here: 339 us
  waiting for transfers between devices  147 us (43%)
  blocking collectives  69.8 us (21%)
  local copies, waits for them, and re-layouts  36.7 us (11%)
  starting transfers between devices  24.2 us (7%)
  matrix products  20 us (6%)
  Pallas kernels  18.9 us (6%)
  between operations  13.3 us (4%)
  other arithmetic  9.1 us (3%)
    all_to_all x1, blocking collectives, per_device(): lax.all_to_all(outgoing.reshape(packed), 'expert', split_axis=0, concat_a...  69.8 us
    all_to_all x2, waiting for transfers between devices, per_device(): lax.all_to_all(served.reshape(packed), 'expert', split_axis=0, concat_axi...  48 us
    reduce_scatter x2, waiting for transfers between devices, expert_rows(): lax.psum_scatter(gate_up(rows, w_gate, w_up), 'dp', scatter_dimension=0,...  41.5 us
    all_to_all x1, waiting for transfers between devices, per_device(): lax.all_to_all(outgoing.reshape(packed), 'expert', split_axis=0, concat_a...  31.3 us
    all_gather x2, waiting for transfers between devices, expert_rows(): lax.all_gather(activated, 'dp', axis=0, tiled=True)  26.2 us
    pallas_call x2, Pallas kernels, gate_up(): pl.pallas_call(gate_up_kernel, grid=(hidden // width,), in_specs=[pl.Bloc...  18.9 us
    all_to_all x2, starting transfers between devices, per_device(): lax.all_to_all(served.reshape(packed), 'expert', split_axis=0, concat_axi...  17.9 us
    dot_general x2, matrix products, expert_rows(): jnp.dot(lax.all_gather(activated, 'dp', axis=0, tiled=True), w_down, pref...  11.4 us
  transfers between devices with their start and end apart: 7, of which 5 were waited for; matrix products, arithmetic and copies ran while one was open for 12% of the time, Pallas kernels for 3%

profile of v5, /device:TPU:1, one launch (start us, length us, event | category | flops | bytes accessed | tf_op | source)
XLA Modules:
  0.0 339.2 jit_solution(9722167458854151835)
XLA Ops:
  6.5 0.0 copy-start
  6.5 0.0 reduce-scatter.3.cloned.1.call-start
  6.5 0.8 copy.15
  7.4 0.1 eq.53
  7.5 0.6 fusion.15
  8.1 0.1 convert_element_type.57
  8.2 0.8 select_reduce_fusion.2
  9.0 0.1 eq.59
  9.1 0.1 add_select_fusion.1
  9.1 1.8 fusion.11
  10.9 0.0 copy-done
  10.9 2.2 convolution_convert_fusion.1
  13.1 4.3 %reshape.37 = bf16[64,140,128]{2,1,0:T(8,128)(2,1)S(1)} reshape(bf16[640,1792]{1,0:T(8,128)(2,1)} %convolution_convert_fusion.1) | data formatting | bytes 4587520 | tf_op jit(solution)/shard_map/reshape | solution.py:87
  17.4 69.8 %all_to_all.20 = bf16[64,140,128]{2,1,0:T(8,128)(2,1)} all-to-all(bf16[64,140,128]{2,1,0:T(8,128)(2,1)S(1)} %reshape.37), channel_id=1, replica_groups=mesh['dp'=4,'expert'=64] {'expert'}, dimensions={0} | all-to-all | bytes 4587520 | tf_op jit(solution)/shard_map/all_to_all | solution.py:87
  87.2 5.1 %reshape.38.x_ref = bf16[640,1792]{1,0:T(8,128)(2,1)} reshape(bf16[64,140,128]{2,1,0:T(8,128)(2,1)} %all_to_all.20) | data formatting | bytes 4587520 | tf_op jit(solution)/shard_map/reshape | solution.py:88
  92.3 9.5 %shard_map.73 = bf16[640,2048]{1,0:T(8,128)(2,1)} custom-call(bf16[640,1792]{1,0:T(8,128)(2,1)} %reshape.38.x_ref, bf16[1792,1024]{1,0:T(8,128)(2,1)} %bitcast.21, bf16[1792,1024]{1,0:T(8,128)(2,1)} %bitcast.23), custom_call_target="tpu_custom_call" | custom-call | tf_op jit(solution)/shard_map/pallas_call | solution.py:23
  101.8 0.0 reduce-scatter.3.cloned.1.call-update
  101.8 0.8 convolution_convert_fusion
  102.6 3.8 %reshape.41 = bf16[64,140,128]{2,1,0:T(8,128)(2,1)} reshape(bf16[640,1792]{1,0:T(8,128)(2,1)S(1)} %convolution_convert_fusion) | data formatting | bytes 4587520 | tf_op jit(solution)/shard_map/reshape | solution.py:87
  106.4 6.0 %all-to-all-start.2 = ((bf16[64,140,128]{2,1,0:T(8,128)(2,1)}), bf16[64,140,128]{2,1,0:T(8,128)(2,1)S(1)}, u32[]{:S(2)}, u32[]{:S(2)}) async-start(bf16[64,140,128]{2,1,0:T(8,128)(2,1)} %reshape.41), calls=%async_computation.3 | async-start | bytes 4718592 | tf_op jit(solution)/shard_map/all_to_all | solution.py:87
  112.4 0.0 all-gather.3.cloned.1.call-start
  112.5 22.8 %reduce-scatter.3.cloned.1.call-done = bf16[160,2048]{1,0:T(8,128)(2,1)} async-done(((bf16[640,2048]{1,0:T(8,128)(2,1)}), bf16[160,2048]{1,0:T(8,128)(2,1)}) %reduce-scatter.3.cloned.1.call-update) | async-done | bytes 655376 | tf_op jit(solution)/shard_map/reduce_scatter | solution.py:37
  135.3 1.2 convert_element_type.60
  136.5 0.9 fusion.17
  137.4 0.0 all-gather.3.cloned.1.call-update
  137.5 0.2 reduce-scatter.5.cloned.1.call-start
  137.7 31.3 %all-to-all-done.2 = bf16[64,140,128]{2,1,0:T(8,128)(2,1)S(1)} async-done(((bf16[64,140,128]{2,1,0:T(8,128)(2,1)}), bf16[64,140,128]{2,1,0:T(8,128)(2,1)S(1)}, u32[]{:S(2)}, u32[]{:S(2)}) %all-to-all-start.2) | async-done | bytes 2293792 | tf_op jit(solution)/shard_map/all_to_all | solution.py:87
  169.0 3.6 %reshape.42.x_ref = bf16[640,1792]{1,0:T(8,128)(2,1)} reshape(bf16[64,140,128]{2,1,0:T(8,128)(2,1)S(1)} %all-to-all-done.2) | data formatting | bytes 4587520 | tf_op jit(solution)/shard_map/reshape | solution.py:88
  172.6 9.5 %shard_map.74 = bf16[640,2048]{1,0:T(8,128)(2,1)} custom-call(bf16[640,1792]{1,0:T(8,128)(2,1)} %reshape.42.x_ref, bf16[1792,1024]{1,0:T(8,128)(2,1)} %bitcast.22, bf16[1792,1024]{1,0:T(8,128)(2,1)} %bitcast.24), custom_call_target="tpu_custom_call" | custom-call | tf_op jit(solution)/shard_map/pallas_call | solution.py:23
  182.0 0.0 reduce-scatter.5.cloned.1.call-update
  182.1 0.0 all-gather.3.cloned.1.call-done
  182.1 5.0 %fusion.5 = bf16[640,1792]{1,0:T(8,128)(2,1)S(1)} fusion(bf16[640,1024]{1,0:T(8,128)(2,1)} %all-gather.3.cloned.1.call-done, bf16[1,1024,1792]{2,1,0:T(8,128)(2,1)} %param.13), kind=kOutput, calls=%fused_computation.6 | convolution fusion | flops 2349957120 | bytes 7274496 | tf_op jit(solution)/shard_map/dot_general | solution.py:44
  187.1 3.8 %reshape.39 = bf16[64,140,128]{2,1,0:T(8,128)(2,1)} reshape(bf16[640,1792]{1,0:T(8,128)(2,1)S(1)} %fusion.5) | data formatting | bytes 4587520 | tf_op jit(solution)/shard_map/reshape | solution.py:89
  190.8 6.0 %all-to-all-start.1 = ((bf16[64,140,128]{2,1,0:T(8,128)(2,1)}), bf16[64,140,128]{2,1,0:T(8,128)(2,1)S(1)}, u32[]{:S(2)}, u32[]{:S(2)}) async-start(bf16[64,140,128]{2,1,0:T(8,128)(2,1)} %reshape.39), calls=%async_computation.2 | async-start | bytes 4718592 | tf_op jit(solution)/shard_map/all_to_all | solution.py:89
  196.8 0.0 all-gather.5.cloned.1.call-start
  196.8 18.6 %reduce-scatter.5.cloned.1.call-done = bf16[160,2048]{1,0:T(8,128)(2,1)} async-done(((bf16[640,2048]{1,0:T(8,128)(2,1)}), bf16[160,2048]{1,0:T(8,128)(2,1)}) %reduce-scatter.5.cloned.1.call-update) | async-done | bytes 655376 | tf_op jit(solution)/shard_map/reduce_scatter | solution.py:37
  215.5 1.2 convert_element_type.67
  216.7 0.9 fusion.16
  217.6 0.0 all-gather.5.cloned.1.call-update
  217.7 26.2 %all-gather.5.cloned.1.call-done = bf16[640,1024]{1,0:T(8,128)(2,1)} async-done(((bf16[160,1024]{1,0:T(8,128)(2,1)}), bf16[640,1024]{1,0:T(8,128)(2,1)}) %all-gather.5.cloned.1.call-update) | async-done | bytes 1310736 | tf_op jit(solution)/shard_map/all_gather | solution.py:45
  243.9 6.4 %fusion.8 = bf16[640,1792]{1,0:T(8,128)(2,1)} fusion(bf16[640,1024]{1,0:T(8,128)(2,1)} %all-gather.5.cloned.1.call-done, bf16[1,1024,1792]{2,1,0:T(8,128)(2,1)} %param.13), kind=kOutput, calls=%fused_computation.7 | convolution fusion | flops 2349957120 | bytes 7274496 | tf_op jit(solution)/shard_map/dot_general | solution.py:44
  250.3 5.3 %reshape.43 = bf16[64,140,128]{2,1,0:T(8,128)(2,1)} reshape(bf16[640,1792]{1,0:T(8,128)(2,1)} %fusion.8) | data formatting | bytes 4587520 | tf_op jit(solution)/shard_map/reshape | solution.py:89
  255.6 0.0 copy-start.2
  255.6 0.0 all-to-all-done.1
  255.6 0.0 copy-start.1
  255.6 1.4 copy-done.1
  257.0 11.9 %all-to-all-start.3 = ((bf16[64,140,128]{2,1,0:T(8,128)(2,1)}), bf16[64,140,128]{2,1,0:T(8,128)(2,1)}, u32[]{:S(2)}, u32[]{:S(2)}) async-start(bf16[64,140,128]{2,1,0:T(8,128)(2,1)} %reshape.43), calls=%async_computation.5 | async-start | bytes 4718592 | tf_op jit(solution)/shard_map/all_to_all | solution.py:89
  269.0 0.0 copy-done.2
  269.0 0.1 copy.18
  269.1 2.2 select_reduce_fusion
  271.3 4.1 %reshape.40 = bf16[640,1792]{1,0:T(8,128)(2,1)S(1)} reshape(bf16[64,140,128]{2,1,0:T(8,128)(2,1)} %copy-done.1) | data formatting | bytes 4587520 | tf_op jit(solution)/shard_map/reshape | solution.py:90
  275.4 0.5 fusion.22
  276.0 1.5 convolution_add_fusion.2
  277.5 48.0 %all-to-all-done.3 = bf16[64,140,128]{2,1,0:T(8,128)(2,1)} async-done(((bf16[64,140,128]{2,1,0:T(8,128)(2,1)}), bf16[64,140,128]{2,1,0:T(8,128)(2,1)}, u32[]{:S(2)}, u32[]{:S(2)}) %all-to-all-start.3) | async-done | bytes 2293792 | tf_op jit(solution)/shard_map/all_to_all | solution.py:89
  325.5 4.1 %reshape.44 = bf16[640,1792]{1,0:T(8,128)(2,1)S(1)} reshape(bf16[64,140,128]{2,1,0:T(8,128)(2,1)} %all-to-all-done.3) | data formatting | bytes 4587520 | tf_op jit(solution)/shard_map/reshape | solution.py:90
  329.7 1.7 convolution_add_fusion.1
  331.4 1.3 fusion.13
  (2 shorter events, 0.0 us)
Async XLA Ops:
  6.5 4.4 %copy-start = (bf16[128,1792]{1,0:T(8,128)(2,1)S(1)}, bf16[128,1792]{1,0:T(8,128)(2,1)}, u32[]{:S(2)}) copy-start(bf16[128,1792]{1,0:T(8,128)(2,1)} %param.7) | copy-start | bytes 1376260
  6.5 128.8 %reduce-scatter.3.cloned.1.call-start = ((), (), s32[]{:S(2)}) async-start(), calls=%async_computation.6 | async-start | bytes 3276800 | tf_op jit(solution)/shard_map/reduce_scatter | solution.py:37
  106.4 62.7 %all-to-all-start.2 = ((bf16[64,140,128]{2,1,0:T(8,128)(2,1)}), bf16[64,140,128]{2,1,0:T(8,128)(2,1)S(1)}, u32[]{:S(2)}, u32[]{:S(2)}) async-start(bf16[64,140,128]{2,1,0:T(8,128)(2,1)} %reshape.41), calls=%async_computation.3 | async-start | bytes 4718592 | tf_op jit(solution)/shard_map/all_to_all | solution.py:87
  112.4 69.7 %all-gather.3.cloned.1.call-start = ((), (), s32[]{:S(2)}) async-start(), calls=%async_computation.7 | async-start | bytes 1638400 | tf_op jit(solution)/shard_map/all_gather | solution.py:45
  137.5 78.0 %reduce-scatter.5.cloned.1.call-start = ((), (), s32[]{:S(2)}) async-start(), calls=%async_computation.8 | async-start | bytes 3276800 | tf_op jit(solution)/shard_map/reduce_scatter | solution.py:37
  190.8 64.8 %all-to-all-start.1 = ((bf16[64,140,128]{2,1,0:T(8,128)(2,1)}), bf16[64,140,128]{2,1,0:T(8,128)(2,1)S(1)}, u32[]{:S(2)}, u32[]{:S(2)}) async-start(bf16[64,140,128]{2,1,0:T(8,128)(2,1)} %reshape.39), calls=%async_computation.2 | async-start | bytes 4718592 | tf_op jit(solution)/shard_map/all_to_all | solution.py:89
  196.8 47.1 %all-gather.5.cloned.1.call-start = ((), (), s32[]{:S(2)}) async-start(), calls=%async_computation.9 | async-start | bytes 1638400 | tf_op jit(solution)/shard_map/all_gather | solution.py:45
  255.6 13.4 %copy-start.2 = (f32[128,8]{0,1:T(8,128)S(1)}, f32[128,8]{0,1:T(8,128)}, u32[]{:S(2)}) copy-start(f32[128,8]{0,1:T(8,128)} %param.9) | copy-start | bytes 12292
  255.6 1.4 copy-start.1
  257.0 68.5 %all-to-all-start.3 = ((bf16[64,140,128]{2,1,0:T(8,128)(2,1)}), bf16[64,140,128]{2,1,0:T(8,128)(2,1)}, u32[]{:S(2)}, u32[]{:S(2)}) async-start(bf16[64,140,128]{2,1,0:T(8,128)(2,1)} %reshape.43), calls=%async_computation.5 | async-start | bytes 4718592 | tf_op jit(solution)/shard_map/all_to_all | solution.py:89
Sparse Core Ops, SparseCore 0:
  101.9 33.3 reduce-scatter.2
  137.6 26.0 all-gather.2
  182.2 33.2 reduce-scatter.4
  217.8 26.0 all-gather.4

commit v6 on v5

--- a/solution.py
+++ b/solution.py
@@ -75,7 +75,8 @@
     lane = 128
     packed = (experts, share * quarter // lane, lane)
     positions = jnp.arange(experts * share, dtype=jnp.int32)
-    mixed = jnp.zeros((tok_rows, quarter), jnp.float32)
+    sent = []
+    hits = []
     for piece in range(pieces):
         inside = (rank_in >= piece * share) & (rank_in < (piece + 1) * share)
         slot_of = jnp.where(inside, home * share + rank_in - piece * share, -1)
@@ -84,11 +85,21 @@
         outgoing = lax.dot_general(
             pick, tokens, (((0,), (0,)), ((), ())), preferred_element_type=jnp.float32
         ).astype(jnp.bfloat16)
-        arrived = lax.all_to_all(outgoing.reshape(packed), "expert", split_axis=0, concat_axis=0, tiled=True)
-        served = expert_rows(arrived.reshape(experts * share, quarter), w_gate, w_up, w_down, hidden)
-        returned = lax.all_to_all(served.reshape(packed), "expert", split_axis=0, concat_axis=0, tiled=True)
+        sent.append(outgoing.reshape(packed))
+        hits.append(hit)
+    arrived = [
+        lax.all_to_all(x, "expert", split_axis=0, concat_axis=0, tiled=True) for x in sent
+    ]
+    mixed = jnp.zeros((tok_rows, quarter), jnp.float32)
+    for piece in range(pieces):
+        served = expert_rows(
+            arrived[piece].reshape(experts * share, quarter), w_gate, w_up, w_down, hidden
+        ).reshape(packed)
+        if piece + 1 < pieces:
+            _, arrived[piece + 1] = lax.optimization_barrier((served, arrived[piece + 1]))
+        returned = lax.all_to_all(served, "expert", split_axis=0, concat_axis=0, tiled=True)
         returned_flat = returned.reshape(experts * share, quarter)
-        weight_of = jnp.sum(jnp.where(hit, route_weights[:, :, None], 0.0), axis=1)
+        weight_of = jnp.sum(jnp.where(hits[piece], route_weights[:, :, None], 0.0), axis=1)
         weight_hi = weight_of.astype(jnp.bfloat16)
         weight_lo = (weight_of - weight_hi.astype(jnp.float32)).astype(jnp.bfloat16)
         mixed = mixed + jnp.dot(weight_hi, returned_flat, preferred_element_type=jnp.float32)

time: 340 us -> 352 us (1.035)
  starting transfers between devices: 24.2 us -> 30 us
    all_to_all x3, waiting for transfers between devices: 79.3 us -> 48 us  [the longest x2 48 us: per_device(): lax.all_to_all(served, 'expert', split_axis=0, concat_axis=0, tiled=True)]
    all_gather x2, waiting for transfers between devices: 26.2 us -> 52.2 us  [expert_rows(): lax.all_gather(activated, 'dp', axis=0, tiled=True)]
    reduce_scatter x2, waiting for transfers between devices: 41.5 us -> 49.3 us  [expert_rows(): lax.psum_scatter(gate_up(rows, w_gate, w_up), 'dp', scatter_dimension=0,...]
    all_to_all x3, starting transfers between devices: 23.9 us -> 29.7 us  [the longest x2 23.7 us: per_device(): lax.all_to_all(served, 'expert', split_axis=0, concat_axis=0, tiled=True)]
  transfers between devices with their start and end apart: 7 -> 7, of which waited for: 5 -> 5; matrix products, arithmetic and copies ran while one was open for 12% -> 12% of each run, Pallas kernels for 3% -> 0%
where the time goes in v6:
time: 352 us; the launch traced here: 350 us
  waiting for transfers between devices  150 us (43%)
  blocking collectives  69.8 us (20%)
  local copies, waits for them, and re-layouts  38.3 us (11%)
  starting transfers between devices  30 us (9%)
  matrix products  21.4 us (6%)
  Pallas kernels  18.9 us (5%)
  between operations  13.3 us (4%)
  other arithmetic  9.1 us (3%)
    all_to_all x1, blocking collectives, per_device(): lax.all_to_all(x, 'expert', split_axis=0, concat_axis=0, tiled=True)  69.8 us
    all_gather x2, waiting for transfers between devices, expert_rows(): lax.all_gather(activated, 'dp', axis=0, tiled=True)  52.2 us
    reduce_scatter x2, waiting for transfers between devices, expert_rows(): lax.psum_scatter(gate_up(rows, w_gate, w_up), 'dp', scatter_dimension=0,...  49.3 us
    all_to_all x2, waiting for transfers between devices, per_device(): lax.all_to_all(served, 'expert', split_axis=0, concat_axis=0, tiled=True)  48 us
    all_to_all x2, starting transfers between devices, per_device(): lax.all_to_all(served, 'expert', split_axis=0, concat_axis=0, tiled=True)  23.7 us
    pallas_call x2, Pallas kernels, gate_up(): pl.pallas_call(gate_up_kernel, grid=(hidden // width,), in_specs=[pl.Bloc...  18.9 us
    dot_general x2, matrix products, expert_rows(): jnp.dot(lax.all_gather(activated, 'dp', axis=0, tiled=True), w_down, pref...  12.8 us
    reshape x2, local copies, waits for them, and re-layouts, per_device(): served = expert_rows(arrived[piece].reshape(experts * share, quarter), w_...  10.6 us
  transfers between devices with their start and end apart: 7, of which 5 were waited for; matrix products, arithmetic and copies ran while one was open for 12% of the time, Pallas kernels for 0%

profile of v6, /device:TPU:1, one launch (start us, length us, event | category | flops | bytes accessed | tf_op | source)
XLA Modules:
  0.0 350.5 jit_solution(10563845530861642116)
XLA Ops:
  6.5 0.0 copy-start
  6.5 0.0 reduce-scatter.3.cloned.1.call-start
  6.5 0.8 copy.15
  7.4 0.1 eq.53
  7.5 0.6 fusion.15
  8.1 0.8 select_reduce_fusion.2
  8.9 0.1 eq.59
  9.0 0.1 convert_element_type.57
  9.1 0.1 add_select_fusion.1
  9.1 1.8 fusion.11
  10.9 0.0 copy-done
  10.9 2.2 convolution_convert_fusion.1
  13.1 4.3 %reshape.37 = bf16[64,140,128]{2,1,0:T(8,128)(2,1)S(1)} reshape(bf16[640,1792]{1,0:T(8,128)(2,1)} %convolution_convert_fusion.1) | data formatting | bytes 4587520 | tf_op jit(solution)/shard_map/reshape | solution.py:88
  17.4 69.8 %all_to_all.20 = bf16[64,140,128]{2,1,0:T(8,128)(2,1)} all-to-all(bf16[64,140,128]{2,1,0:T(8,128)(2,1)S(1)} %reshape.37), channel_id=1, replica_groups=mesh['dp'=4,'expert'=64] {'expert'}, dimensions={0} | all-to-all | bytes 4587520 | tf_op jit(solution)/shard_map/all_to_all | solution.py:91
  87.2 5.1 %reshape.38.x_ref = bf16[640,1792]{1,0:T(8,128)(2,1)} reshape(bf16[64,140,128]{2,1,0:T(8,128)(2,1)} %all_to_all.20) | data formatting | bytes 4587520 | tf_op jit(solution)/shard_map/reshape | solution.py:96
  92.3 9.5 %shard_map.73 = bf16[640,2048]{1,0:T(8,128)(2,1)} custom-call(bf16[640,1792]{1,0:T(8,128)(2,1)} %reshape.38.x_ref, bf16[1792,1024]{1,0:T(8,128)(2,1)} %bitcast.21, bf16[1792,1024]{1,0:T(8,128)(2,1)} %bitcast.23), custom_call_target="tpu_custom_call" | custom-call | tf_op jit(solution)/shard_map/pallas_call | solution.py:23
  101.8 0.0 reduce-scatter.3.cloned.1.call-update
  101.8 0.8 convolution_convert_fusion
  102.6 3.8 %reshape.41 = bf16[64,140,128]{2,1,0:T(8,128)(2,1)} reshape(bf16[640,1792]{1,0:T(8,128)(2,1)S(1)} %convolution_convert_fusion) | data formatting | bytes 4587520 | tf_op jit(solution)/shard_map/reshape | solution.py:88
  106.4 6.0 %all-to-all-start.2 = ((bf16[64,140,128]{2,1,0:T(8,128)(2,1)}), bf16[64,140,128]{2,1,0:T(8,128)(2,1)S(1)}, u32[]{:S(2)}, u32[]{:S(2)}) async-start(bf16[64,140,128]{2,1,0:T(8,128)(2,1)} %reshape.41), calls=%async_computation.3 | async-start | bytes 4718592 | tf_op jit(solution)/shard_map/all_to_all | solution.py:91
  112.4 0.0 all-gather.3.cloned.1.call-start
  112.5 22.8 %reduce-scatter.3.cloned.1.call-done = bf16[160,2048]{1,0:T(8,128)(2,1)} async-done(((bf16[640,2048]{1,0:T(8,128)(2,1)}), bf16[160,2048]{1,0:T(8,128)(2,1)}) %reduce-scatter.3.cloned.1.call-update) | async-done | bytes 655376 | tf_op jit(solution)/shard_map/reduce_scatter | solution.py:37
  135.3 1.2 convert_element_type.60
  136.5 0.9 fusion.17
  137.4 0.0 all-gather.3.cloned.1.call-update
  137.5 0.2 reduce-scatter.5.cloned.1.call-start
  137.7 26.0 %all-gather.3.cloned.1.call-done = bf16[640,1024]{1,0:T(8,128)(2,1)} async-done(((bf16[160,1024]{1,0:T(8,128)(2,1)}), bf16[640,1024]{1,0:T(8,128)(2,1)}) %all-gather.3.cloned.1.call-update) | async-done | bytes 1310736 | tf_op jit(solution)/shard_map/all_gather | solution.py:45
  163.7 6.4 %fusion.5 = bf16[640,1792]{1,0:T(8,128)(2,1)} fusion(bf16[640,1024]{1,0:T(8,128)(2,1)} %all-gather.3.cloned.1.call-done, bf16[1,1024,1792]{2,1,0:T(8,128)(2,1)} %param.13), kind=kOutput, calls=%fused_computation.6 | convolution fusion | flops 2349957120 | bytes 7274496 | tf_op jit(solution)/shard_map/dot_general | solution.py:44
  170.1 5.3 %reshape.39 = bf16[64,140,128]{2,1,0:T(8,128)(2,1)} reshape(bf16[640,1792]{1,0:T(8,128)(2,1)} %fusion.5) | data formatting | bytes 4587520 | tf_op jit(solution)/shard_map/reshape | solution.py:97
  175.4 0.0 all-to-all-done.2
  175.4 3.6 %reshape.42.x_ref = bf16[640,1792]{1,0:T(8,128)(2,1)} reshape(bf16[64,140,128]{2,1,0:T(8,128)(2,1)S(1)} %all-to-all-done.2) | data formatting | bytes 4587520 | tf_op jit(solution)/shard_map/reshape | solution.py:96
  179.0 9.5 %shard_map.74 = bf16[640,2048]{1,0:T(8,128)(2,1)} custom-call(bf16[640,1792]{1,0:T(8,128)(2,1)} %reshape.42.x_ref, bf16[1792,1024]{1,0:T(8,128)(2,1)} %bitcast.22, bf16[1792,1024]{1,0:T(8,128)(2,1)} %bitcast.24), custom_call_target="tpu_custom_call" | custom-call | tf_op jit(solution)/shard_map/pallas_call | solution.py:23
  188.4 0.0 reduce-scatter.5.cloned.1.call-update
  188.4 11.8 %all-to-all-start.1 = ((bf16[64,140,128]{2,1,0:T(8,128)(2,1)}), bf16[64,140,128]{2,1,0:T(8,128)(2,1)S(1)}, u32[]{:S(2)}, u32[]{:S(2)}) async-start(bf16[64,140,128]{2,1,0:T(8,128)(2,1)} %reshape.39), calls=%async_computation.2 | async-start | bytes 4718592 | tf_op jit(solution)/shard_map/all_to_all | solution.py:100
  200.2 0.0 all-gather.5.cloned.1.call-start
  200.3 26.5 %reduce-scatter.5.cloned.1.call-done = bf16[160,2048]{1,0:T(8,128)(2,1)} async-done(((bf16[640,2048]{1,0:T(8,128)(2,1)}), bf16[160,2048]{1,0:T(8,128)(2,1)}) %reduce-scatter.5.cloned.1.call-update) | async-done | bytes 655376 | tf_op jit(solution)/shard_map/reduce_scatter | solution.py:37
  226.8 1.2 convert_element_type.67
  228.0 0.9 fusion.16
  228.9 0.0 all-gather.5.cloned.1.call-update
  228.9 26.2 %all-gather.5.cloned.1.call-done = bf16[640,1024]{1,0:T(8,128)(2,1)} async-done(((bf16[160,1024]{1,0:T(8,128)(2,1)}), bf16[640,1024]{1,0:T(8,128)(2,1)}) %all-gather.5.cloned.1.call-update) | async-done | bytes 1310736 | tf_op jit(solution)/shard_map/all_gather | solution.py:45
  255.1 6.4 %fusion.8 = bf16[640,1792]{1,0:T(8,128)(2,1)} fusion(bf16[640,1024]{1,0:T(8,128)(2,1)} %all-gather.5.cloned.1.call-done, bf16[1,1024,1792]{2,1,0:T(8,128)(2,1)} %param.13), kind=kOutput, calls=%fused_computation.7 | convolution fusion | flops 2349957120 | bytes 7274496 | tf_op jit(solution)/shard_map/dot_general | solution.py:44
  261.5 5.3 %reshape.43 = bf16[64,140,128]{2,1,0:T(8,128)(2,1)} reshape(bf16[640,1792]{1,0:T(8,128)(2,1)} %fusion.8) | data formatting | bytes 4587520 | tf_op jit(solution)/shard_map/reshape | solution.py:97
  266.9 0.0 copy-start.2
  266.9 0.0 all-to-all-done.1
  266.9 0.0 copy-start.1
  266.9 1.4 copy-done.1
  268.3 11.9 %all-to-all-start.3 = ((bf16[64,140,128]{2,1,0:T(8,128)(2,1)}), bf16[64,140,128]{2,1,0:T(8,128)(2,1)}, u32[]{:S(2)}, u32[]{:S(2)}) async-start(bf16[64,140,128]{2,1,0:T(8,128)(2,1)} %reshape.43), calls=%async_computation.5 | async-start | bytes 4718592 | tf_op jit(solution)/shard_map/all_to_all | solution.py:100
  280.3 0.0 copy-done.2
  280.3 0.1 copy.18
  280.4 2.2 select_reduce_fusion
  282.6 4.1 %reshape.40 = bf16[640,1792]{1,0:T(8,128)(2,1)S(1)} reshape(bf16[64,140,128]{2,1,0:T(8,128)(2,1)} %copy-done.1) | data formatting | bytes 4587520 | tf_op jit(solution)/shard_map/reshape | solution.py:101
  286.7 0.5 fusion.22
  287.3 1.5 convolution_add_fusion.2
  288.8 48.0 %all-to-all-done.3 = bf16[64,140,128]{2,1,0:T(8,128)(2,1)} async-done(((bf16[64,140,128]{2,1,0:T(8,128)(2,1)}), bf16[64,140,128]{2,1,0:T(8,128)(2,1)}, u32[]{:S(2)}, u32[]{:S(2)}) %all-to-all-start.3) | async-done | bytes 2293792 | tf_op jit(solution)/shard_map/all_to_all | solution.py:100
  336.8 4.1 %reshape.44 = bf16[640,1792]{1,0:T(8,128)(2,1)S(1)} reshape(bf16[64,140,128]{2,1,0:T(8,128)(2,1)} %all-to-all-done.3) | data formatting | bytes 4587520 | tf_op jit(solution)/shard_map/reshape | solution.py:101
  340.9 1.7 convolution_add_fusion.1
  342.6 1.3 fusion.13
  (2 shorter events, 0.0 us)
Async XLA Ops:
  6.5 4.4 %copy-start = (bf16[128,1792]{1,0:T(8,128)(2,1)S(1)}, bf16[128,1792]{1,0:T(8,128)(2,1)}, u32[]{:S(2)}) copy-start(bf16[128,1792]{1,0:T(8,128)(2,1)} %param.7) | copy-start | bytes 1376260
  6.5 128.8 %reduce-scatter.3.cloned.1.call-start = ((), (), s32[]{:S(2)}) async-start(), calls=%async_computation.6 | async-start | bytes 3276800 | tf_op jit(solution)/shard_map/reduce_scatter | solution.py:37
  106.4 69.0 %all-to-all-start.2 = ((bf16[64,140,128]{2,1,0:T(8,128)(2,1)}), bf16[64,140,128]{2,1,0:T(8,128)(2,1)S(1)}, u32[]{:S(2)}, u32[]{:S(2)}) async-start(bf16[64,140,128]{2,1,0:T(8,128)(2,1)} %reshape.41), calls=%async_computation.3 | async-start | bytes 4718592 | tf_op jit(solution)/shard_map/all_to_all | solution.py:91
  112.4 51.3 %all-gather.3.cloned.1.call-start = ((), (), s32[]{:S(2)}) async-start(), calls=%async_computation.7 | async-start | bytes 1638400 | tf_op jit(solution)/shard_map/all_gather | solution.py:45
  137.5 89.3 %reduce-scatter.5.cloned.1.call-start = ((), (), s32[]{:S(2)}) async-start(), calls=%async_computation.8 | async-start | bytes 3276800 | tf_op jit(solution)/shard_map/reduce_scatter | solution.py:37
  188.4 78.4 %all-to-all-start.1 = ((bf16[64,140,128]{2,1,0:T(8,128)(2,1)}), bf16[64,140,128]{2,1,0:T(8,128)(2,1)S(1)}, u32[]{:S(2)}, u32[]{:S(2)}) async-start(bf16[64,140,128]{2,1,0:T(8,128)(2,1)} %reshape.39), calls=%async_computation.2 | async-start | bytes 4718592 | tf_op jit(solution)/shard_map/all_to_all | solution.py:100
  200.2 54.9 %all-gather.5.cloned.1.call-start = ((), (), s32[]{:S(2)}) async-start(), calls=%async_computation.9 | async-start | bytes 1638400 | tf_op jit(solution)/shard_map/all_gather | solution.py:45
  266.9 13.4 %copy-start.2 = (f32[128,8]{0,1:T(8,128)S(1)}, f32[128,8]{0,1:T(8,128)}, u32[]{:S(2)}) copy-start(f32[128,8]{0,1:T(8,128)} %param.9) | copy-start | bytes 12292
  266.9 1.4 copy-start.1
  268.3 68.5 %all-to-all-start.3 = ((bf16[64,140,128]{2,1,0:T(8,128)(2,1)}), bf16[64,140,128]{2,1,0:T(8,128)(2,1)}, u32[]{:S(2)}, u32[]{:S(2)}) async-start(bf16[64,140,128]{2,1,0:T(8,128)(2,1)} %reshape.43), calls=%async_computation.5 | async-start | bytes 4718592 | tf_op jit(solution)/shard_map/all_to_all | solution.py:100
Sparse Core Ops, SparseCore 0:
  101.9 33.3 reduce-scatter.2
  137.6 26.0 all-gather.2
  188.6 38.1 reduce-scatter.4
  229.1 26.0 all-gather.4

commit v7 on v5

--- a/solution.py
+++ b/solution.py
@@ -70,23 +70,27 @@
     home = jnp.where(flag == 1, (flat_ids + experts // 2) % experts, flat_ids)
     home = home.reshape(tok_rows, choices_per)
     rank_in = rank_in.reshape(tok_rows, choices_per)
-    pieces = 2 if capacity % 2 == 0 else 1
-    share = capacity // pieces
     lane = 128
-    packed = (experts, share * quarter // lane, lane)
-    positions = jnp.arange(experts * share, dtype=jnp.int32)
+    first = capacity // 16 * 16
+    bounds = [(0, first), (first, capacity)] if 0 < first < capacity else [(0, capacity)]
     mixed = jnp.zeros((tok_rows, quarter), jnp.float32)
-    for piece in range(pieces):
-        inside = (rank_in >= piece * share) & (rank_in < (piece + 1) * share)
-        slot_of = jnp.where(inside, home * share + rank_in - piece * share, -1)
+    for low, high in bounds:
+        share = high - low
+        if share % 16 == 0:
+            layout = (experts, share, quarter)
+        else:
+            layout = (experts, share * quarter // lane, lane)
+        positions = jnp.arange(experts * share, dtype=jnp.int32)
+        inside = (rank_in >= low) & (rank_in < high)
+        slot_of = jnp.where(inside, home * share + rank_in - low, -1)
         hit = slot_of[:, :, None] == positions[None, None, :]
         pick = jnp.any(hit, axis=1).astype(jnp.bfloat16)
         outgoing = lax.dot_general(
             pick, tokens, (((0,), (0,)), ((), ())), preferred_element_type=jnp.float32
         ).astype(jnp.bfloat16)
-        arrived = lax.all_to_all(outgoing.reshape(packed), "expert", split_axis=0, concat_axis=0, tiled=True)
+        arrived = lax.all_to_all(outgoing.reshape(layout), "expert", split_axis=0, concat_axis=0, tiled=True)
         served = expert_rows(arrived.reshape(experts * share, quarter), w_gate, w_up, w_down, hidden)
-        returned = lax.all_to_all(served.reshape(packed), "expert", split_axis=0, concat_axis=0, tiled=True)
+        returned = lax.all_to_all(served.reshape(layout), "expert", split_axis=0, concat_axis=0, tiled=True)
         returned_flat = returned.reshape(experts * share, quarter)
         weight_of = jnp.sum(jnp.where(hit, route_weights[:, :, None], 0.0), axis=1)
         weight_hi = weight_of.astype(jnp.bfloat16)

time: 340 us -> 358 us (1.053)
  blocking collectives: 69.8 us -> 140 us
  local copies, waits for them, and re-layouts: 36.7 us -> 7.28 us
  waiting for transfers between devices: 147 us -> 128 us
    all_to_all x1 -> x2, blocking collectives: 69.8 us -> 129 us  [per_device(): lax.all_to_all(outgoing.reshape(layout), 'expert', split_axis=0, concat_a...]
    all_gather x2 -> x1, waiting for transfers between devices: 26.2 us -> 4.74 us  [expert_rows(): lax.all_gather(activated, 'dp', axis=0, tiled=True)]
    all_to_all x3 -> x2, waiting for transfers between devices: 79.3 us -> 94.3 us  [per_device(): lax.all_to_all(served.reshape(layout), 'expert', split_axis=0, concat_axi...]
    reshape x4 -> x2, local copies, waits for them, and re-layouts: 17.1 us -> 3.08 us  [the longest x1 2.02 us: per_device(): served.reshape(layout)]
    reduce_scatter x2, waiting for transfers between devices: 41.5 us -> 29 us  [expert_rows(): lax.psum_scatter(gate_up(rows, w_gate, w_up), 'dp', scatter_dimension=0,...]
    all_gather x0 -> x1, blocking collectives: none -> 10.9 us  [expert_rows(): lax.all_gather(activated, 'dp', axis=0, tiled=True)]
    reshape x2 -> x1, local copies, waits for them, and re-layouts: 8.26 us -> 1.03 us  [per_device(): returned_flat = returned.reshape(experts * share, quarter)]
    reshape x2 -> x1, local copies, waits for them, and re-layouts: 8.7 us -> 1.95 us  [per_device(): arrived.reshape(experts * share, quarter)]
  transfers between devices with their start and end apart: 7 -> 5, of which waited for: 5 -> 5; matrix products, arithmetic and copies ran while one was open for 12% -> 7% of each run, Pallas kernels for 3% -> 2%
where the time goes in v7:
time: 358 us
  blocking collectives  140 us (39%)
  waiting for transfers between devices  128 us (36%)
  starting transfers between devices  21.1 us (6%)
  matrix products  20.5 us (6%)
  Pallas kernels  19.5 us (5%)
  between operations  13.3 us (4%)
  other arithmetic  7.88 us (2%)
  local copies, waits for them, and re-layouts  7.28 us (2%)
    all_to_all x2, blocking collectives, per_device(): lax.all_to_all(outgoing.reshape(layout), 'expert', split_axis=0, concat_a...  129 us
    all_to_all x2, waiting for transfers between devices, per_device(): lax.all_to_all(served.reshape(layout), 'expert', split_axis=0, concat_axi...  94.3 us
    reduce_scatter x2, waiting for transfers between devices, expert_rows(): lax.psum_scatter(gate_up(rows, w_gate, w_up), 'dp', scatter_dimension=0,...  29 us
    all_to_all x2, starting transfers between devices, per_device(): lax.all_to_all(served.reshape(layout), 'expert', split_axis=0, concat_axi...  21 us
    pallas_call x2, Pallas kernels, gate_up(): pl.pallas_call(gate_up_kernel, grid=(hidden // width,), in_specs=[pl.Bloc...  19.5 us
    dot_general x2, matrix products, expert_rows(): jnp.dot(lax.all_gather(activated, 'dp', axis=0, tiled=True), w_down, pref...  11.6 us
    all_gather x1, blocking collectives, expert_rows(): lax.all_gather(activated, 'dp', axis=0, tiled=True)  10.9 us
  transfers between devices with their start and end apart: 5, of which 5 were waited for; matrix products, arithmetic and copies ran while one was open for 7% of the time, Pallas kernels for 2%

profile of v7, /device:TPU:1, one launch (start us, length us, event | category | flops | bytes accessed | tf_op | source)
XLA Modules:
  0.0 357.8 jit_solution(4884816828882902384)
XLA Ops:
  6.5 0.0 copy-start
  6.5 0.0 reduce-scatter.3.cloned.1.call-start
  6.5 0.8 copy.17
  7.4 0.1 eq.53
  7.5 0.6 fusion.10
  8.1 0.1 convert_element_type.57
  8.2 0.8 select_reduce_fusion.2
  9.0 0.1 eq.59
  9.1 0.1 add_select_fusion.1
  9.1 1.3 fusion
  10.5 0.0 copy-done
  10.5 1.2 convolution_convert_fusion
  11.6 97.6 %all_to_all.20 = bf16[64,16,1792]{2,1,0:T(8,128)(2,1)} all-to-all(bf16[64,16,1792]{2,1,0:T(8,128)(2,1)S(1)} %bitcast.23), channel_id=1, replica_groups=mesh['dp'=4,'expert'=64] {'expert'}, dimensions={0} | all-to-all | bytes 7340032 | tf_op jit(solution)/shard_map/all_to_all | solution.py:91
  109.2 13.1 %shard_map.73 = bf16[1024,2048]{1,0:T(8,128)(2,1)} custom-call(bf16[1024,1792]{1,0:T(8,128)(2,1)} %bitcast.28, bf16[1792,1024]{1,0:T(8,128)(2,1)} %bitcast.24, bf16[1792,1024]{1,0:T(8,128)(2,1)} %bitcast.26), custom_call_target="tpu_custom_call" | custom-call | tf_op jit(solution)/shard_map/pallas_call | solution.py:23
  122.4 0.0 reduce-scatter.3.cloned.1.call-update
  122.4 0.0 reduce-scatter.5.cloned.1.call-start
  122.4 0.4 fusion.12
  122.8 0.4 convolution_convert_fusion.2
  123.3 1.1 reshape.41
  124.4 31.6 %all_to_all.21 = bf16[64,56,128]{2,1,0:T(8,128)(2,1)S(1)} all-to-all(bf16[64,56,128]{2,1,0:T(8,128)(2,1)S(1)} %reshape.41), channel_id=1, replica_groups=mesh['dp'=4,'expert'=64] {'expert'}, dimensions={0} | all-to-all | bytes 1835008 | tf_op jit(solution)/shard_map/all_to_all | solution.py:91
  156.0 2.0 reshape.42.x_ref
  157.9 6.3 %shard_map.74 = bf16[256,2048]{1,0:T(8,128)(2,1)} custom-call(bf16[256,1792]{1,0:T(8,128)(2,1)} %reshape.42.x_ref, bf16[1792,1024]{1,0:T(8,128)(2,1)} %bitcast.25, bf16[1792,1024]{1,0:T(8,128)(2,1)} %bitcast.27), custom_call_target="tpu_custom_call" | custom-call | tf_op jit(solution)/shard_map/pallas_call | solution.py:23
  164.3 0.0 reduce-scatter.5.cloned.1.call-update
  164.3 0.0 all-gather.2.cloned.1.call-start
  164.4 4.4 %reduce-scatter.3.cloned.1.call-done = bf16[256,2048]{1,0:T(8,128)(2,1)} async-done(((bf16[1024,2048]{1,0:T(8,128)(2,1)}), bf16[256,2048]{1,0:T(8,128)(2,1)}) %reduce-scatter.3.cloned.1.call-update) | async-done | bytes 1048592 | tf_op jit(solution)/shard_map/reduce_scatter | solution.py:37
  168.8 1.5 convert_element_type.60
  170.2 1.1 fusion.11
  171.3 0.0 all-gather.2.cloned.1.call-update
  171.4 24.6 %reduce-scatter.5.cloned.1.call-done = bf16[64,2048]{1,0:T(8,128)(2,1)} async-done(((bf16[256,2048]{1,0:T(8,128)(2,1)}), bf16[64,2048]{1,0:T(8,128)(2,1)}) %reduce-scatter.5.cloned.1.call-update) | async-done | bytes 262160 | tf_op jit(solution)/shard_map/reduce_scatter | solution.py:37
  196.0 1.0 convert_element_type.67
  197.0 0.1 fusion.13
  197.0 10.9 %all_gather.7 = bf16[256,1024]{1,0:T(8,128)(2,1)S(1)} all-gather(bf16[64,1024]{1,0:T(8,128)(2,1)S(1)} %fusion.13), channel_id=1, replica_groups=mesh['dp'=4,'expert'=64] {'dp'}, dimensions={0}, use_global_device_ids=true | all-gather | bytes 655360 | tf_op jit(solution)/shard_map/all_gather | solution.py:45
  207.9 3.1 fusion.5
  211.1 2.0 reshape.43
  213.1 14.5 %all-to-all-start.3 = ((bf16[64,56,128]{2,1,0:T(8,128)(2,1)}), bf16[64,56,128]{2,1,0:T(8,128)(2,1)S(1)}, u32[]{:S(2)}, u32[]{:S(2)}) async-start(bf16[64,56,128]{2,1,0:T(8,128)(2,1)} %reshape.43), calls=%async_computation.5 | async-start | bytes 1835008 | tf_op jit(solution)/shard_map/all_to_all | solution.py:93
  227.6 4.7 %all-gather.2.cloned.1.call-done = bf16[1024,1024]{1,0:T(8,128)(2,1)} async-done(((bf16[256,1024]{1,0:T(8,128)(2,1)}), bf16[1024,1024]{1,0:T(8,128)(2,1)}) %all-gather.2.cloned.1.call-update) | async-done | bytes 2097168 | tf_op jit(solution)/shard_map/all_gather | solution.py:45
  232.3 8.4 %convolution_convert_fusion.1 = bf16[1024,1792]{1,0:T(8,128)(2,1)} fusion(bf16[1024,1024]{1,0:T(8,128)(2,1)} %all-gather.2.cloned.1.call-done, bf16[1,1024,1792]{2,1,0:T(8,128)(2,1)} %param.13), kind=kOutput, calls=%fused_computation.6 | convolution fusion | flops 3759931392 | bytes 9437184 | tf_op jit(solution)/shard_map/dot_general | solution.py:44
  240.7 12.6 %all-to-all-done.3 = bf16[64,56,128]{2,1,0:T(8,128)(2,1)S(1)} async-done(((bf16[64,56,128]{2,1,0:T(8,128)(2,1)}), bf16[64,56,128]{2,1,0:T(8,128)(2,1)S(1)}, u32[]{:S(2)}, u32[]{:S(2)}) %all-to-all-start.3) | async-done | bytes 917536 | tf_op jit(solution)/shard_map/all_to_all | solution.py:93
  253.3 0.0 copy-start.1
  253.3 6.5 %all-to-all-start.1 = ((bf16[64,16,1792]{2,1,0:T(8,128)(2,1)}), bf16[64,16,1792]{2,1,0:T(8,128)(2,1)}, u32[]{:S(2)}, u32[]{:S(2)}) async-start(bf16[64,16,1792]{2,1,0:T(8,128)(2,1)} %bitcast.29), calls=%async_computation.2 | async-start | bytes 7340032 | tf_op jit(solution)/shard_map/all_to_all | solution.py:93
  259.8 0.0 copy-done.1
  259.8 0.1 copy.20
  259.9 0.4 select_reduce_fusion.1
  260.3 1.3 select_reduce_fusion
  261.6 1.0 reshape.44
  262.7 81.8 %all-to-all-done.1 = bf16[64,16,1792]{2,1,0:T(8,128)(2,1)} async-done(((bf16[64,16,1792]{2,1,0:T(8,128)(2,1)}), bf16[64,16,1792]{2,1,0:T(8,128)(2,1)}, u32[]{:S(2)}, u32[]{:S(2)}) %all-to-all-start.1) | async-done | bytes 3670048 | tf_op jit(solution)/shard_map/all_to_all | solution.py:93
  344.4 2.7 fusion.15
  347.1 2.7 convolution_add_fusion.2
  349.9 0.3 convolution_add_fusion.1
  350.2 1.1 fusion.8
  (2 shorter events, 0.0 us)
Async XLA Ops:
  6.5 3.9 %copy-start = (bf16[128,1792]{1,0:T(8,128)(2,1)S(1)}, bf16[128,1792]{1,0:T(8,128)(2,1)}, u32[]{:S(2)}) copy-start(bf16[128,1792]{1,0:T(8,128)(2,1)} %param.7) | copy-start | bytes 1376260
  6.5 162.2 %reduce-scatter.3.cloned.1.call-start = ((), (), s32[]{:S(2)}) async-start(), calls=%async_computation.6 | async-start | bytes 5242880 | tf_op jit(solution)/shard_map/reduce_scatter | solution.py:37
  122.4 73.6 %reduce-scatter.5.cloned.1.call-start = ((), (), s32[]{:S(2)}) async-start(), calls=%async_computation.8 | async-start | bytes 1310720 | tf_op jit(solution)/shard_map/reduce_scatter | solution.py:37
  164.3 68.0 %all-gather.2.cloned.1.call-start = ((), (), s32[]{:S(2)}) async-start(), calls=%async_computation.7 | async-start | bytes 2621440 | tf_op jit(solution)/shard_map/all_gather | solution.py:45
  213.1 40.2 %all-to-all-start.3 = ((bf16[64,56,128]{2,1,0:T(8,128)(2,1)}), bf16[64,56,128]{2,1,0:T(8,128)(2,1)S(1)}, u32[]{:S(2)}, u32[]{:S(2)}) async-start(bf16[64,56,128]{2,1,0:T(8,128)(2,1)} %reshape.43), calls=%async_computation.5 | async-start | bytes 1835008 | tf_op jit(solution)/shard_map/all_to_all | solution.py:93
  253.3 6.5 %copy-start.1 = (f32[128,8]{0,1:T(8,128)S(1)}, f32[128,8]{0,1:T(8,128)}, u32[]{:S(2)}) copy-start(f32[128,8]{0,1:T(8,128)} %param.9) | copy-start | bytes 12292
  253.3 91.2 %all-to-all-start.1 = ((bf16[64,16,1792]{2,1,0:T(8,128)(2,1)}), bf16[64,16,1792]{2,1,0:T(8,128)(2,1)}, u32[]{:S(2)}, u32[]{:S(2)}) async-start(bf16[64,16,1792]{2,1,0:T(8,128)(2,1)} %bitcast.29), calls=%async_computation.2 | async-start | bytes 7340032 | tf_op jit(solution)/shard_map/all_to_all | solution.py:93
Sparse Core Ops, SparseCore 0:
  122.5 46.2 reduce-scatter.2
  171.3 24.5 reduce-scatter.4
  197.8 34.4 all-gather.1
